TPU v7x, 32 devices: a whole 2x2x4 slice. The times are simulated.
32 devices in a mesh: task: 8 (over y, x, core), samp: 4 (over z).
Axes of the slice: x: 2, y: 2, z: 4, core: 2. Of those that a mesh axis runs over, the one named last changes fastest.
Arguments:
- cells: bfloat16 [8, 512, 4, 512], P('task', 'samp'), may hold values from -6 to 6
- out_grad: bfloat16 [8, 512, 4, 512], P('task', 'samp'), may hold values from -6 to 6
- sample_counts: int32 [8], P('task'), may hold values from 51 to 512, as said below
- feature_counts: int32 [8], P('task'), may hold values from 2 to 4, as said below
- sample_block: float32 [1049088], P(('task', 'samp'))
- sample_first: float32 [1049088], P(('task', 'samp'))
- sample_second: float32 [1049088], P(('task', 'samp')), as said below
- feature_block: float32 [1049088], P(('task', 'samp'))
- feature_first: float32 [1049088], P(('task', 'samp'))
- feature_second: float32 [1049088], P(('task', 'samp')), as said below
- mlp_block: float32 [2097664], P(('task', 'samp'))
- mlp_first: float32 [2097664], P(('task', 'samp'))
- mlp_second: float32 [2097664], P(('task', 'samp')), as said below
Outputs:
- layer_out: bfloat16 [8, 512, 4, 512], P('task', 'samp')
- cells_grad: float32 [8, 512, 4, 512], P('task', 'samp')
- sample_grad: float32 [1049088], P(('task', 'samp'))
- sample_first_new: float32 [1049088], P(('task', 'samp'))
- sample_second_new: float32 [1049088], P(('task', 'samp'))
- sample_master_new: float32 [1049088], P(('task', 'samp'))
- sample_weights_new: bfloat16 [1049088], P(('task', 'samp'))
- feature_grad: float32 [1049088], P(('task', 'samp'))
- feature_first_new: float32 [1049088], P(('task', 'samp'))
- feature_second_new: float32 [1049088], P(('task', 'samp'))
- feature_master_new: float32 [1049088], P(('task', 'samp'))
- feature_weights_new: bfloat16 [1049088], P(('task', 'samp'))
- mlp_grad: float32 [2097664], P(('task', 'samp'))
- mlp_first_new: float32 [2097664], P(('task', 'samp'))
- mlp_second_new: float32 [2097664], P(('task', 'samp'))
- mlp_master_new: float32 [2097664], P(('task', 'samp'))
- mlp_weights_new: bfloat16 [2097664], P(('task', 'samp'))
- norm_pairs: float32 [9, 2], replicated
Inputs may be any that keep to these rules, and one draw needn't show every extreme that they name: `sample_counts`: samples at or beyond a task's count are padding; some task fills all 512 slots. `feature_counts`: features at or beyond a task's count are padding; some task fills all 4 slots. `sample_second`: every entry is positive. `feature_second`: every entry is positive. `mlp_second`: every entry is positive.
All inputs are finite; a program needn't handle non-finite values.
Results may differ from a plain program's by a relative error of at most 0.025.
The roundings to bfloat16 on the way count: a program that leaves them out, or rounds other values in their place, can miss the bound.
Values may be sent and summed in bfloat16 or wider, within the bound.
A program may use at most 128 MiB of HBM per device.

v0:
```python
import jax
import jax.numpy as jnp
from jax import lax
from jax.experimental import pallas as pl
from jax.experimental.pallas import tpu as pltpu
from jax.sharding import PartitionSpec as P

D = 512
HEADS = 8
HEAD_DIM = 64
FF = 2048


EPS_NORM = 1e-05
EPS_ADAM = 1e-06
STEP_RATE = 0.5
BIG_NEGATIVE = -1e30


def normalize(hidden, gain_row):
    centre = jnp.mean(hidden, -1, keepdims=True)
    shifted = hidden - centre
    spread = jnp.mean(shifted * shifted, -1, keepdims=True)
    return shifted * lax.rsqrt(spread + EPS_NORM) * gain_row


def norm_backward(hidden, gain_row, normed_grad):
    _, pullback = jax.vjp(normalize, hidden, gain_row)
    return pullback(normed_grad)


def gelu_exact(upward):
    return jax.nn.gelu(upward, approximate=False)


def contract_rows(left, right):
    return lax.dot_general(
        left, right, (((0,), (0,)), ((), ())), preferred_element_type=jnp.float32
    )


def times_transpose(left, right):
    return lax.dot_general(
        left, right, (((1,), (1,)), ((), ())), preferred_element_type=jnp.float32
    )


def unpack(flat_params, width_in, width_mid):
    gain_row = flat_params[:D].astype(jnp.float32)
    w_in = flat_params[D : D + D * width_in].reshape(D, width_in)
    w_out = flat_params[D + D * width_in :].reshape(width_mid, D)
    return (gain_row, w_in, w_out)


def fetch_forward(master):
    return lax.all_gather(master.astype(jnp.bfloat16), ("task", "samp"), axis=0, tiled=True)


def fetch_again(master):
    return lax.all_gather(master.astype(jnp.bfloat16), ("task", "samp"), axis=0, tiled=True)


def reduce_grads(gain_grad, in_grad, out_grad_matrix):
    flat_grads = jnp.concatenate([gain_grad, in_grad.reshape(-1), out_grad_matrix.reshape(-1)])
    return lax.psum_scatter(flat_grads, ("task", "samp"), scatter_dimension=0, tiled=True)


def group_size(feature_total, most):
    chosen = 1
    for candidate in range(1, most + 1):
        if feature_total % candidate == 0:
            chosen = candidate
    return chosen


def lamb_prepare(grad_shard, master, first, second, width_in):
    first_new = 0.5 * first + 0.5 * grad_shard
    second_new = 0.5 * second + 0.5 * grad_shard * grad_shard
    direction = first_new / (jnp.sqrt(second_new) + EPS_ADAM)
    entries = master.shape[0]
    position = lax.axis_index(("task", "samp")) * entries + jnp.arange(entries, dtype=jnp.int32)
    segment = (position >= D).astype(jnp.int32) + (position >= D + D * width_in).astype(jnp.int32)
    member = segment[None, :] == jnp.arange(3, dtype=jnp.int32)[:, None]
    weight_sums = jnp.sum(jnp.where(member, (master * master)[None, :], 0.0), 1)
    update_sums = jnp.sum(jnp.where(member, (direction * direction)[None, :], 0.0), 1)
    return (first_new, second_new, direction, member, jnp.stack([weight_sums, update_sums], 1))


def lamb_finish(master, block_state, trust_ratio):
    factor = jnp.sum(jnp.where(block_state[3], trust_ratio[:, None], 0.0), 0)
    return master - STEP_RATE * factor * block_state[2]


def sample_scores(query_part, key_part, key_live, score_scale):
    scores = (
        jnp.einsum("qfhe,kfhe->fhqk", query_part, key_part, preferred_element_type=jnp.float32)
        * score_scale
    )
    return jnp.where(key_live, scores, BIG_NEGATIVE)


def sample_forward(queries, pairs_all, key_live, block_features, score_scale):
    local_rows, features = (queries.shape[0], queries.shape[1])

    def one_block(block_index, results):
        attended, log_totals = results
        offset = block_index * block_features
        query_part = lax.dynamic_slice_in_dim(queries, offset, block_features, 1)
        pair_part = lax.dynamic_slice_in_dim(pairs_all, offset, block_features, 1)
        scores = sample_scores(query_part, pair_part[:, :, 0], key_live, score_scale)
        row_top = jnp.max(scores, -1, keepdims=True)
        exponent = jnp.exp(scores - row_top)
        row_total = jnp.sum(exponent, -1, keepdims=True)
        probability = (exponent / row_total).astype(jnp.bfloat16)
        block_out = jnp.einsum(
            "fhqk,kfhe->qfhe", probability, pair_part[:, :, 1], preferred_element_type=jnp.float32
        )
        attended = lax.dynamic_update_slice_in_dim(
            attended, block_out.astype(jnp.bfloat16), offset, 1
        )
        log_totals = lax.dynamic_update_slice_in_dim(
            log_totals, (row_top + jnp.log(row_total))[..., 0], offset, 0
        )
        return (attended, log_totals)

    start_state = (
        jnp.zeros(queries.shape, jnp.bfloat16),
        jnp.zeros((features, HEADS, local_rows), jnp.float32),
    )
    return lax.fori_loop(0, features // block_features, one_block, start_state)


def query_side(query_part, pair_part, grad_part, log_part, key_live, score_scale):
    key_part = pair_part[:, :, 0]
    value_part = pair_part[:, :, 1]
    scores = sample_scores(query_part, key_part, key_live, score_scale)
    probability = jnp.exp(scores - log_part[..., None])
    prob_grad = jnp.einsum(
        "qfhe,kfhe->fhqk", grad_part, value_part, preferred_element_type=jnp.float32
    )
    row_inner = jnp.sum(probability * prob_grad, -1, keepdims=True)
    score_grad = (probability * (prob_grad - row_inner)).astype(jnp.bfloat16)
    query_block = (
        jnp.einsum("fhqk,kfhe->qfhe", score_grad, key_part, preferred_element_type=jnp.float32)
        * score_scale
    )
    return (probability, score_grad, row_inner, query_block)


def sample_backward(
    queries, pairs_all, key_live, log_totals, attended_grad, block_features, score_scale
):
    local_rows, features = (queries.shape[0], queries.shape[1])

    def one_block(block_index, results):
        query_grads, pair_grads = results
        offset = block_index * block_features
        query_part = lax.dynamic_slice_in_dim(queries, offset, block_features, 1)
        pair_part = lax.dynamic_slice_in_dim(pairs_all, offset, block_features, 1)
        grad_part = lax.dynamic_slice_in_dim(attended_grad, offset, block_features, 1)
        log_part = lax.dynamic_slice_in_dim(log_totals, offset, block_features, 0)
        probability, score_grad, row_inner, query_block = query_side(
            query_part, pair_part, grad_part, log_part, key_live, score_scale
        )
        key_block = (
            jnp.einsum(
                "fhqk,qfhe->kfhe", score_grad, query_part, preferred_element_type=jnp.float32
            )
            * score_scale
        )
        value_block = jnp.einsum(
            "fhqk,qfhe->kfhe",
            probability.astype(jnp.bfloat16),
            grad_part,
            preferred_element_type=jnp.float32,
        )
        pair_terms = jnp.stack([key_block, value_block], 2)
        pair_local = lax.psum_scatter(
            pair_terms.astype(jnp.bfloat16), "samp", scatter_dimension=0, tiled=True
        ).astype(jnp.float32)
        query_grads = lax.dynamic_update_slice_in_dim(query_grads, query_block, offset, 1)
        pair_grads = lax.dynamic_update_slice_in_dim(pair_grads, pair_local, offset, 1)
        return (query_grads, pair_grads)

    start_state = (
        jnp.zeros((local_rows, features, HEADS, HEAD_DIM), jnp.float32),
        jnp.zeros((local_rows, features, 2, HEADS, HEAD_DIM), jnp.float32),
    )
    return lax.fori_loop(0, features // block_features, one_block, start_state)


def on_device(
    cells,
    out_grad,
    sample_counts,
    feature_counts,
    sample_block,
    sample_first,
    sample_second,
    feature_block,
    feature_first,
    feature_second,
    mlp_block,
    mlp_first,
    mlp_second,
):
    local_rows, features = (cells.shape[1], cells.shape[2])
    flat_rows = local_rows * features
    seq_all = local_rows * lax.axis_size("samp")
    score_scale = HEAD_DIM ** (-0.5)
    block_features = group_size(features, max(1, 2048 // (HEADS * local_rows)))
    sample_index = lax.axis_index("samp") * local_rows + jnp.arange(local_rows, dtype=jnp.int32)
    sample_live = sample_index < sample_counts[0]
    key_live = jnp.arange(seq_all, dtype=jnp.int32) < sample_counts[0]
    feature_live = jnp.arange(features, dtype=jnp.int32) < feature_counts[0]
    cell_live = sample_live[:, None, None] & feature_live[None, :, None]
    hidden_in = cells[0].astype(jnp.float32)
    gain_one, in_one, out_one = unpack(fetch_forward(sample_block), 3 * D, D)
    normed_one = normalize(hidden_in, gain_one).astype(jnp.bfloat16)
    packed_one = jnp.dot(
        normed_one.reshape(flat_rows, D), in_one, preferred_element_type=jnp.float32
    )
    packed_one = packed_one.astype(jnp.bfloat16).reshape(local_rows, features, 3, HEADS, HEAD_DIM)
    queries_one = packed_one[:, :, 0]
    pairs_local = packed_one[:, :, 1:]
    pairs_all = lax.all_gather(pairs_local, "samp", axis=0, tiled=True)
    attended_one, log_totals = sample_forward(
        queries_one, pairs_all, key_live, block_features, score_scale
    )
    attended_one_rows = attended_one.reshape(flat_rows, D)
    branch_one = jnp.dot(attended_one_rows, out_one, preferred_element_type=jnp.float32)
    hidden_one = hidden_in + branch_one.reshape(local_rows, features, D)
    gain_two, in_two, out_two = unpack(fetch_forward(feature_block), 3 * D, D)
    normed_two = normalize(hidden_one, gain_two).astype(jnp.bfloat16).reshape(flat_rows, D)
    packed_two = jnp.dot(normed_two, in_two, preferred_element_type=jnp.float32)
    packed_two = packed_two.astype(jnp.bfloat16).reshape(local_rows, features, 3, HEADS, HEAD_DIM)
    queries_two, key_two, value_two = (
        packed_two[:, :, 0],
        packed_two[:, :, 1],
        packed_two[:, :, 2],
    )
    scores_two = (
        jnp.einsum("sqhe,skhe->shqk", queries_two, key_two, preferred_element_type=jnp.float32)
        * score_scale
    )
    scores_two = jnp.where(feature_live, scores_two, BIG_NEGATIVE)
    row_top = jnp.max(scores_two, -1, keepdims=True)
    exponent = jnp.exp(scores_two - row_top)
    probability_two = exponent / jnp.sum(exponent, -1, keepdims=True)
    prob_low_two = probability_two.astype(jnp.bfloat16)
    attended_two = jnp.einsum(
        "shqk,skhe->sqhe", prob_low_two, value_two, preferred_element_type=jnp.float32
    )
    attended_two_rows = attended_two.reshape(flat_rows, D).astype(jnp.bfloat16)
    branch_two = jnp.dot(attended_two_rows, out_two, preferred_element_type=jnp.float32)
    hidden_two = hidden_one + branch_two.reshape(local_rows, features, D)
    gain_three, up_weight, down_weight = unpack(fetch_forward(mlp_block), FF, FF)
    normed_three = normalize(hidden_two, gain_three).astype(jnp.bfloat16).reshape(flat_rows, D)
    upward = jnp.dot(normed_three, up_weight, preferred_element_type=jnp.float32)
    activated = gelu_exact(upward).astype(jnp.bfloat16)
    branch_three = jnp.dot(activated, down_weight, preferred_element_type=jnp.float32)
    hidden_three = hidden_two + branch_three.reshape(local_rows, features, D)
    layer_out = jnp.where(cell_live, hidden_three, 0.0).astype(jnp.bfloat16)[None]
    top_grad = jnp.where(cell_live, out_grad[0], jnp.zeros((), jnp.bfloat16))
    top_rows = top_grad.reshape(flat_rows, D)
    gain_three, up_weight, down_weight = unpack(fetch_again(mlp_block), FF, FF)
    down_grad = contract_rows(activated, top_rows)
    act_grad = times_transpose(top_rows, down_weight).astype(jnp.bfloat16)
    _, gelu_pull = jax.vjp(gelu_exact, upward)
    up_grad = gelu_pull(act_grad.astype(jnp.float32))[0].astype(jnp.bfloat16)
    upw_grad = contract_rows(normed_three, up_grad)
    normed_grad = times_transpose(up_grad, up_weight).reshape(local_rows, features, D)
    hidden_grad, gain_three_grad = norm_backward(hidden_two, gain_three, normed_grad)
    grad_two = top_grad.astype(jnp.float32) + hidden_grad
    mlp_shard = reduce_grads(gain_three_grad, upw_grad, down_grad)
    mlp_state = lamb_prepare(mlp_shard, mlp_block, mlp_first, mlp_second, FF)
    gain_two, in_two, out_two = unpack(fetch_again(feature_block), 3 * D, D)
    branch_grad = grad_two.astype(jnp.bfloat16).reshape(flat_rows, D)
    out_two_grad = contract_rows(attended_two_rows, branch_grad)
    attended_grad = (
        times_transpose(branch_grad, out_two)
        .astype(jnp.bfloat16)
        .reshape(local_rows, features, HEADS, HEAD_DIM)
    )
    prob_grad = jnp.einsum(
        "sqhe,skhe->shqk", attended_grad, value_two, preferred_element_type=jnp.float32
    )
    row_inner = jnp.sum(probability_two * prob_grad, -1, keepdims=True)
    score_grad = (probability_two * (prob_grad - row_inner)).astype(jnp.bfloat16)
    query_grad = (
        jnp.einsum("shqk,skhe->sqhe", score_grad, key_two, preferred_element_type=jnp.float32)
        * score_scale
    )
    key_grad = (
        jnp.einsum("shqk,sqhe->skhe", score_grad, queries_two, preferred_element_type=jnp.float32)
        * score_scale
    )
    value_grad = jnp.einsum(
        "shqk,sqhe->skhe", prob_low_two, attended_grad, preferred_element_type=jnp.float32
    )
    packed_grad = (
        jnp.stack([query_grad, key_grad, value_grad], 2)
        .astype(jnp.bfloat16)
        .reshape(flat_rows, 3 * D)
    )
    in_two_grad = contract_rows(normed_two, packed_grad)
    normed_grad = times_transpose(packed_grad, in_two).reshape(local_rows, features, D)
    hidden_grad, gain_two_grad = norm_backward(hidden_one, gain_two, normed_grad)
    grad_one = grad_two + hidden_grad
    feature_shard = reduce_grads(gain_two_grad, in_two_grad, out_two_grad)
    feature_state = lamb_prepare(feature_shard, feature_block, feature_first, feature_second, 3 * D)
    gain_one, in_one, out_one = unpack(fetch_again(sample_block), 3 * D, D)
    pairs_all = lax.all_gather(pairs_local, "samp", axis=0, tiled=True)
    branch_grad = grad_one.astype(jnp.bfloat16).reshape(flat_rows, D)
    out_one_grad = contract_rows(attended_one_rows, branch_grad)
    attended_grad = (
        times_transpose(branch_grad, out_one)
        .astype(jnp.bfloat16)
        .reshape(local_rows, features, HEADS, HEAD_DIM)
    )
    query_grads, pair_grads = sample_backward(
        queries_one, pairs_all, key_live, log_totals, attended_grad, block_features, score_scale
    )
    packed_grad = (
        jnp.concatenate([query_grads[:, :, None], pair_grads], 2)
        .astype(jnp.bfloat16)
        .reshape(flat_rows, 3 * D)
    )
    in_one_grad = contract_rows(normed_one.reshape(flat_rows, D), packed_grad)
    normed_grad = times_transpose(packed_grad, in_one).reshape(local_rows, features, D)
    hidden_grad, gain_one_grad = norm_backward(hidden_in, gain_one, normed_grad)
    cells_grad = (grad_one + hidden_grad)[None]
    sample_shard = reduce_grads(gain_one_grad, in_one_grad, out_one_grad)
    sample_state = lamb_prepare(sample_shard, sample_block, sample_first, sample_second, 3 * D)
    totals = lax.psum(
        jnp.concatenate([sample_state[4], feature_state[4], mlp_state[4]], 0), ("task", "samp")
    )
    norm_pairs = jnp.sqrt(totals)
    trust_ratio = norm_pairs[:, 0] / (norm_pairs[:, 1] + EPS_ADAM)
    sample_master = lamb_finish(sample_block, sample_state, trust_ratio[0:3])
    feature_master = lamb_finish(feature_block, feature_state, trust_ratio[3:6])
    mlp_master = lamb_finish(mlp_block, mlp_state, trust_ratio[6:9])
    return (
        layer_out,
        cells_grad,
        sample_shard,
        sample_state[0],
        sample_state[1],
        sample_master,
        sample_master.astype(jnp.bfloat16),
        feature_shard,
        feature_state[0],
        feature_state[1],
        feature_master,
        feature_master.astype(jnp.bfloat16),
        mlp_shard,
        mlp_state[0],
        mlp_state[1],
        mlp_master,
        mlp_master.astype(jnp.bfloat16),
        norm_pairs,
    )


D = 512
MESH = pl.DeviceIdType.MESH
BF = jnp.bfloat16
F32 = jnp.float32
NEG = -1e30


def mult(value, factor):
    return pl.multiple_of(value, factor)


def nt(left, right):
    return lax.dot_general(left, right, (((1,), (1,)), ((), ())), preferred_element_type=F32)


def nn(left, right):
    return lax.dot_general(left, right, (((1,), (0,)), ((), ())), preferred_element_type=F32)


def here():
    return lax.axis_index("task"), lax.axis_index("samp")


def peers(t, s):
    return (
        (jnp.bitwise_xor(t, 1), s),
        (jnp.bitwise_xor(t, 2), s),
        (jnp.bitwise_xor(t, 4), s),
        (t, (s + 1) % 4),
        (t, (s + 2) % 4),
        (t, (s + 3) % 4),
    )


def enter(t, s):
    barrier = pltpu.get_barrier_semaphore()
    for peer in peers(t, s):
        pl.semaphore_signal(barrier, inc=1, device_id=peer, device_id_type=MESH)
    return barrier


def send(src, dst, ssem, rsem, peer):
    copy = pltpu.make_async_remote_copy(
        src_ref=src, dst_ref=dst, send_sem=ssem, recv_sem=rsem, device_id=peer, device_id_type=MESH
    )
    copy.start()
    return copy


class Gather:
    def __init__(self, buf, half, ssem, rsem, t, s):
        self.buf, self.t, self.s = buf, t, s
        rows = buf.shape[1]
        self.ha, self.hb = pl.ds(0, half), pl.ds(half, rows - half)
        self.all = pl.ds(0, rows)
        self.ssem, self.rsem = ssem, rsem
        self.count = 0
        self.copies = []
        self.tx, self.ty = jnp.bitwise_xor(t, 2), jnp.bitwise_xor(t, 4)
        self.txy, self.tc = jnp.bitwise_xor(t, 6), jnp.bitwise_xor(t, 1)

    def go(self, slots, rows, peer):
        view = self.buf.at[slots, rows]
        i = self.count
        self.count += 1
        copy = send(view, view, self.ssem.at[i], self.rsem.at[i], peer)
        self.copies.append(copy)
        return copy

    def four(self, t):
        return pl.ds(4 * t, 4)

    def z(self):
        t, s = self.t, self.s
        own = pl.ds(4 * t + s, 1)
        self.zc = [self.go(own, self.all, (t, (s + k) % 4)) for k in (1, 2, 3)]

    def one(self):
        for copy in self.zc:
            copy.wait_recv()
        t, s = self.t, self.s
        self.x1 = self.go(self.four(t), self.ha, (self.tx, s))
        self.y1 = self.go(self.four(t), self.hb, (self.ty, s))
        self.c = [self.go(self.four(t), self.all, (self.tc, s))]

    def two(self):
        s = self.s
        t = self.t
        self.x1.wait_recv()
        self.y2 = [
            self.go(self.four(t), self.ha, (self.ty, s)),
            self.go(self.four(self.tx), self.ha, (self.ty, s)),
        ]
        self.y1.wait_recv()
        self.x2 = [
            self.go(self.four(t), self.hb, (self.tx, s)),
            self.go(self.four(self.ty), self.hb, (self.tx, s)),
        ]
        self.c.append(self.go(self.four(self.tx), self.ha, (self.tc, s)))
        self.c.append(self.go(self.four(self.ty), self.hb, (self.tc, s)))

    def three(self):
        s = self.s
        for copy in self.y2 + self.x2:
            copy.wait_recv()
        self.c.append(self.go(self.four(self.ty), self.ha, (self.tc, s)))
        self.c.append(self.go(self.four(self.txy), self.ha, (self.tc, s)))
        self.c.append(self.go(self.four(self.tx), self.hb, (self.tc, s)))
        self.c.append(self.go(self.four(self.txy), self.hb, (self.tc, s)))

    def end(self):
        for copy in self.c:
            copy.wait_recv()

    def drain(self):
        for copy in self.copies:
            copy.wait_send()


def realign(m_ref, sh_ref, d, rows, out_ref, out_at, roll_to):
    whole = 4 * rows
    total = whole + 8
    q, p = d // 8, d % 8
    lane = lax.broadcasted_iota(jnp.int32, (total, 128), 1)
    roll_to[0:8, :] = jnp.zeros((8, 128), F32)
    for i in range(whole // 8):
        sh_ref[8 * i : 8 * i + 8, :] = m_ref[pl.ds(1024 * i, 1024)].reshape(8, 128)
    sh_ref[whole:total, :] = jnp.zeros((8, 128), F32)
    sh_ref[whole : whole + 1, 0:16] = m_ref[pl.ds(128 * whole, 16)].reshape(1, 16)
    rolled = pltpu.roll(sh_ref[0:total, :], 16 * p, 1)
    roll_to[8 : 8 + total, :] = rolled
    sh_ref[0:8, :] = jnp.zeros((8, 128), F32)
    sh_ref[8 : 8 + total, :] = jnp.where(lane < 16 * p, roll_to[7 : 7 + total, :], rolled)
    firsts = []
    for b in range(4):
        out_ref[out_at, 0:rows, 128 * b : 128 * b + 128] = sh_ref[pl.ds(12 - q + b, rows, stride=4), :].astype(BF)
        firsts.append(sh_ref[pl.ds(8 - q + b, 1), :])
    return jnp.concatenate(firsts, 1)


def spread(buf, firsts, kind, rows, lo, hi, put):
    tail = lax.broadcasted_iota(jnp.int32, (8, D), 0) == 7

    def body(i, _):
        nxt = jnp.minimum(i + 1, 31)
        row = firsts[nxt, 64:80, :].astype(F32)[kind : kind + 1, :]
        block = buf[i, 0:rows, :].astype(F32)
        last = block[rows - 8 : rows, :] + jnp.where(tail & (i < 31), row, 0.0)
        put(i - lo, block[0 : rows - 8, :], last)
        return 0

    lax.fori_loop(lo, hi, body, 0)


def put_f32(dst, rows):
    def put(i, head, last):
        for b in range(4):
            cols = slice(128 * b, 128 * b + 128)
            dst[b, pl.ds(mult(i * rows, rows), rows - 8), :] = head[:, cols]
            dst[b, pl.ds(mult(i * rows + rows - 8, 8), 8), :] = last[:, cols]

    return put


def put_bf(dst, rows):
    def put(i, head, last):
        dst[pl.ds(mult(i * rows, rows), rows), :] = jnp.concatenate([head, last], 0).astype(BF)

    return put


def split_columns(wide, ways, dst):
    def body(i, _):
        for j in range(ways):
            for b in range(4):
                piece = wide[b, pl.ds(64 * ways * i + j, 64, stride=ways), :]
                dst[j, pl.ds(mult(64 * i, 64), 64), 128 * b : 128 * b + 128] = piece.astype(BF)
        return 0

    lax.fori_loop(0, 8, body, 0)


def halves():
    lane = lax.broadcasted_iota(jnp.int32, (128, 128), 1)
    return lane < 64


def attend_chunk(qkv, c, live, out):
    left = halves()
    one = jnp.where(left, 0.125, 0.0).astype(BF)
    two = jnp.where(left, 0.0, 0.125).astype(BF)

    def body(h, _):
        cols = pl.ds(mult(h * 128, 128), 128)
        q = qkv[0, pl.ds(mult(c * 128, 128), 128), cols]
        qm = jnp.concatenate([q * one, q * two], 0)
        scores = jnp.where(live, nt(qm, qkv[1, :, cols]), NEG)
        top = jnp.max(scores, 1, keepdims=True)
        e = jnp.exp(scores - top)
        prob = (e * (1.0 / jnp.sum(e, 1, keepdims=True))).astype(BF)
        o = nn(prob, qkv[2, :, cols])
        o = jnp.where(left, o[0:128], o[128:256]).astype(BF)
        for g in range(4):
            out[g, :, cols] = o[32 * g : 32 * g + 32]
        return 0

    lax.fori_loop(0, 4, body, 0)


def kernel_a(
    cnt, cells, m1, m2, m3,
    o1rows, w1, wo1, w2, wo2, wup, wdn, gains, qkv, a1, cf,
    g1, g2, g3, wide, sh, ro, o1c, w1v, wo1v, w2v, wo2v, wupv, wdnv, qkvv,
    gs, gr, as_, ar, os_, or_, lsem,
):
    t, s = here()
    d = 4 * t + s
    barrier = enter(t, s)
    ga = Gather(g1, 32, gs.at[0], gr.at[0], t, s)
    gb = Gather(g2, 32, gs.at[1], gr.at[1], t, s)
    gc = Gather(g3, 64, gs.at[2], gr.at[2], t, s)
    f1 = realign(m1, sh, d, 64, g1, d, ro)
    f2 = realign(m2, sh, d, 64, g2, d, ro)
    f3 = realign(m3, sh, d, 128, g3, d, ro)
    row = lax.broadcasted_iota(jnp.int32, (16, D), 0)
    firsts = jnp.where(row == 0, f1, jnp.where(row == 1, f2, jnp.where(row == 2, f3, 0.0)))
    g1[d, 64:80, :] = firsts.astype(BF)
    pl.semaphore_wait(barrier, 6)
    ga.z()
    cf[s] = cells[:, s, :, :]
    moves = [
        send(cells.at[:, (s + k) % 4], cf.at[s], as_.at[k - 1], ar.at[k - 1], (t, (s + k) % 4)) for k in (1, 2, 3)
    ]
    ga.one()
    ga.two()
    for copy in moves:
        copy.wait_recv()
    gb.z()
    gc.z()
    ga.three()
    ga.end()
    spread(g1, g1, 0, 64, 0, 24, put_f32(wide, 64))
    split_columns(wide, 3, w1v)
    spread(g1, g1, 0, 64, 24, 32, put_bf(wo1v, 64))
    gains[...] = g1[0, 64:80, :].astype(F32)[0:8]
    gain = g1[0, 64:80, :].astype(F32)[0:1]

    def norm(i, _):
        h = cf[i].astype(F32).reshape(128, D)
        mean = jnp.mean(h, 1, keepdims=True)
        x = h - mean
        var = jnp.mean(x * x, 1, keepdims=True)
        a1[pl.ds(mult(i * 128, 128), 128), :] = (x * lax.rsqrt(var + 1e-5) * gain).astype(BF)
        return 0

    lax.fori_loop(0, 4, norm, 0)

    def project(i, _):
        j, r = i // 4, i % 4
        rows = pl.ds(mult(r * 128, 128), 128)
        qkvv[j, rows, :] = nn(a1[rows, :], w1v[j]).astype(BF)
        return 0

    lax.fori_loop(0, 12, project, 0)
    live = lax.broadcasted_iota(jnp.int32, (1, 512), 1) < cnt[0]
    backs = []
    local = []

    def keep(src, dst):
        copy = pltpu.make_async_copy(src, dst, lsem.at[len(local)])
        copy.start()
        local.append(copy)

    keep(w1v, w1)
    keep(wo1v, wo1)
    keep(qkvv, qkv)
    for k in (2, 1, 3, 0):
        c = (s + k) % 4
        if k:
            attend_chunk(qkvv, c, live, o1c.at[k - 1])
            backs.append(send(o1c.at[k - 1], o1rows.at[:, s], os_.at[k - 1], or_.at[k - 1], (t, c)))
        else:
            attend_chunk(qkvv, c, live, o1rows.at[:, s])
        if k == 2:
            gb.one()
            gc.one()
        if k == 1:
            gb.two()
            gc.two()
        if k == 3:
            gb.three()
    gb.end()
    spread(g2, g1, 1, 64, 0, 24, put_f32(wide, 64))
    split_columns(wide, 3, w2v)
    spread(g2, g1, 1, 64, 24, 32, put_bf(wo2v, 64))
    keep(w2v, w2)
    keep(wo2v, wo2)
    gc.three()
    gc.end()
    spread(g3, g1, 2, 128, 0, 16, put_f32(wide, 128))
    split_columns(wide, 4, wupv)
    keep(wupv, wup)
    spread(g3, g1, 2, 128, 16, 32, put_bf(wdnv, 128))
    keep(wdnv, wdn)
    for copy in backs:
        copy.wait_recv()
    for copy in moves + backs:
        copy.wait_send()
    ga.drain()
    gb.drain()
    gc.drain()
    for copy in local:
        copy.wait()


def call_a(cnt, cells_fm, m1, m2, m3):
    sds = jax.ShapeDtypeStruct
    vm = pl.BlockSpec(memory_space=pltpu.VMEM)
    hb = pl.BlockSpec(memory_space=pl.ANY)
    return pl.pallas_call(
        kernel_a,
        name="kernel_a",
        out_shape=(
            sds((4, 4, 32, D), BF), sds((3, D, D), BF), sds((D, D), BF), sds((3, D, D), BF), sds((D, D), BF),
            sds((4, D, D), BF), sds((4 * D, D), BF), sds((8, D), F32), sds((3, D, D), BF), sds((D, D), BF),
            sds((4, 4, 32, D), BF),
        ),
        in_specs=[pl.BlockSpec(memory_space=pltpu.SMEM), vm, vm, vm, vm],
        out_specs=(vm, hb, hb, hb, hb, hb, hb, vm, hb, vm, vm),
        scratch_shapes=[
            pltpu.VMEM((32, 80, D), BF), pltpu.VMEM((32, 64, D), BF), pltpu.VMEM((32, 128, D), BF),
            pltpu.VMEM((4, 4 * D, 128), F32), pltpu.VMEM((536, 128), F32), pltpu.VMEM((536, 128), F32),
            pltpu.VMEM((3, 4, 32, D), BF),
            pltpu.VMEM((3, D, D), BF), pltpu.VMEM((D, D), BF), pltpu.VMEM((3, D, D), BF), pltpu.VMEM((D, D), BF),
            pltpu.VMEM((4, D, D), BF), pltpu.VMEM((4 * D, D), BF), pltpu.VMEM((3, D, D), BF),
            pltpu.SemaphoreType.DMA((3, 16)), pltpu.SemaphoreType.DMA((3, 16)),
            pltpu.SemaphoreType.DMA((3,)), pltpu.SemaphoreType.DMA((3,)),
            pltpu.SemaphoreType.DMA((3,)), pltpu.SemaphoreType.DMA((3,)),
            pltpu.SemaphoreType.DMA((7,)),
        ],
        compiler_params=pltpu.CompilerParams(collective_id=1, has_side_effects=True, vmem_limit_bytes=56 << 20),
    )(cnt, cells_fm, m1, m2, m3)


def edges(d, entries, width):
    begin = d * entries
    return D - begin, D + D * width - begin


def segment(k, ends):
    return (k >= ends[0]).astype(jnp.int32) + (k >= ends[1]).astype(jnp.int32)


def lamb_step(g, m, f, s):
    fn = 0.5 * f + 0.5 * g
    sn = 0.5 * s + 0.5 * g * g
    return fn, sn, fn / (jnp.sqrt(sn) + 1e-6)


def squares(sh, m, f, s, sums, d, width, b):
    entries = m.shape[0]
    whole = entries // 1024
    ends = edges(d, entries, width)
    lane = lax.broadcasted_iota(jnp.int32, (8, 128), 0) * 128 + lax.broadcasted_iota(jnp.int32, (8, 128), 1)
    zero = jnp.zeros((8, 128), F32)

    def body(i, acc):
        at = pl.ds(mult(i * 1024, 1024), 1024)
        old = m[at].reshape(8, 128)
        _, _, r = lamb_step(
            sh[pl.ds(mult(i * 8, 8), 8), :], old, f[at].reshape(8, 128), s[at].reshape(8, 128)
        )
        part = segment(lane + i * 1024, ends)
        out = []
        for n, value in enumerate((old * old, r * r)):
            for k in range(3):
                out.append(acc[3 * n + k] + jnp.where(part == k, value, 0.0))
        return tuple(out)

    acc = lax.fori_loop(0, whole, body, (zero,) * 6)
    at = pl.ds(whole * 1024, 16)
    old = m[at].reshape(1, 16)
    _, _, r = lamb_step(
        sh[8 * whole : 8 * whole + 1, 0:16], old, f[at].reshape(1, 16), s[at].reshape(1, 16)
    )
    part = segment(lax.broadcasted_iota(jnp.int32, (1, 16), 1) + whole * 1024, ends)
    first = lax.broadcasted_iota(jnp.int32, (1, 128), 1) == 0
    for n, value in enumerate((old * old, r * r)):
        for k in range(3):
            row = 16 * n + 3 * b + k
            tail = jnp.sum(jnp.where(part == k, value, 0.0), 1, keepdims=True)
            sums[row : row + 1, :] = jnp.sum(acc[3 * n + k], 0, keepdims=True) + jnp.where(first, tail, 0.0)


def update(sh, m, f, s, grad, fout, sout, mout, wout, ratio, d, width, b):
    entries = m.shape[0]
    whole = entries // 1024
    ends = edges(d, entries, width)
    half = [0.5 * ratio[3 * b + k : 3 * b + k + 1, :] for k in range(3)]

    def put(at, g, part, shape):
        old = m[at].reshape(shape)
        fn, sn, r = lamb_step(g, old, f[at].reshape(shape), s[at].reshape(shape))
        factor = jnp.where(part == 0, half[0], jnp.where(part == 1, half[1], half[2]))
        new = (old - factor * r).reshape(-1)
        grad[at] = g.reshape(-1)
        fout[at] = fn.reshape(-1)
        sout[at] = sn.reshape(-1)
        mout[at] = new
        wout[at] = new.astype(BF)

    lane = lax.broadcasted_iota(jnp.int32, (8, 128), 0) * 128 + lax.broadcasted_iota(jnp.int32, (8, 128), 1)

    def body(i, _):
        at = pl.ds(mult(i * 1024, 1024), 1024)
        put(at, sh[pl.ds(mult(i * 8, 8), 8), :], segment(lane + i * 1024, ends), (8, 128))
        return 0

    lax.fori_loop(0, whole, body, 0)
    part = segment(lax.broadcasted_iota(jnp.int32, (1, 16), 1) + whole * 1024, ends)
    put(pl.ds(whole * 1024, 16), sh[8 * whole : 8 * whole + 1, 0:16], part, (1, 16))


def sum_all(sums, got, zs, ssem, rsem, t, s):
    copies = []
    for i, e in enumerate((1, 2, 4)):
        copy = send(sums.at[i], got.at[i], ssem.at[i], rsem.at[i], (jnp.bitwise_xor(t, e), s))
        copies.append(copy)
        copy.wait_recv()
        if i < 2:
            sums[i + 1] = sums[i] + got[i]
        else:
            zs[s] = sums[i] + got[i]
    last = [
        send(zs.at[s], zs.at[s], ssem.at[2 + k], rsem.at[2 + k], (t, (s + k) % 4)) for k in (1, 2, 3)
    ]
    for copy in last:
        copy.wait_recv()
    return zs[0] + zs[1] + zs[2] + zs[3], copies + last


def kernel_e(
    total, sh1, sh2, sh3, m1, f1, s1, m2, f2, s2, m3, f3, s3,
    g1, fo1, so1, mo1, wo1, g2, fo2, so2, mo2, wo2, g3, fo3, so3, mo3, wo3, pairs,
):
    t, s = here()
    d = 4 * t + s
    norm = jnp.sqrt(jnp.sum(total[...], 1, keepdims=True))
    pairs[...] = jnp.concatenate([norm[0:9], norm[16:25]], 1)
    ratio = norm[0:9] / (norm[16:25] + 1e-6)
    update(sh1, m1, f1, s1, g1, fo1, so1, mo1, wo1, ratio, d, 3 * D, 0)
    update(sh2, m2, f2, s2, g2, fo2, so2, mo2, wo2, ratio, d, 3 * D, 1)
    update(sh3, m3, f3, s3, g3, fo3, so3, mo3, wo3, ratio, d, 4 * D, 2)


def call_e(total, shards, args):
    sds = jax.ShapeDtypeStruct
    vm = pl.BlockSpec(memory_space=pltpu.VMEM)
    shapes = []
    for m in args[0::3]:
        n = m.shape
        shapes += [sds(n, F32)] * 4 + [sds(n, BF)]
    return pl.pallas_call(
        kernel_e,
        name="kernel_e",
        out_shape=(*shapes, sds((9, 2), F32)),
        in_specs=[vm] * 13,
        out_specs=(vm,) * 16,
        compiler_params=pltpu.CompilerParams(vmem_limit_bytes=40 << 20),
    )(total, *shards, *args)


class Scatter:
    def __init__(self, part, r1, acc, ry, rx, ry2, rx2, rz, half, ssem, rsem, t, s):
        self.part, self.r1, self.acc = part, r1, acc
        self.ry, self.rx, self.ry2, self.rx2, self.rz = ry, rx, ry2, rx2, rz
        self.rows = part.shape[1]
        self.ha, self.hb = half, self.rows - half
        self.ssem, self.rsem, self.t, self.s = ssem, rsem, t, s
        self.count = 0
        self.copies = []

    def go(self, src, dst, peer):
        i = self.count
        self.count += 1
        copy = send(src, dst, self.ssem.at[i], self.rsem.at[i], peer)
        self.copies.append(copy)
        return copy

    def xor(self, e):
        return jnp.bitwise_xor(self.t, e)

    def core(self):
        tc = self.xor(1)
        self.c = [
            self.go(self.part.at[pl.ds(4 * jnp.bitwise_xor(tc, 2 * e), 4)], self.r1.at[e], (tc, self.s))
            for e in (2, 3, 1, 0)
        ]

    def core_sum(self):
        for n, e in enumerate((2, 3, 1, 0)):
            self.c[n].wait_recv()
            base = 4 * self.xor(2 * e)

            def body(j, _, e=e, base=base):
                own = self.part[base + j, :, :].astype(F32)
                self.acc[e, j, :, :] = (own + self.r1[e, j, :, :].astype(F32)).astype(BF)
                return 0

            lax.fori_loop(0, 4, body, 0)

    def one(self):
        ha, hb = pl.ds(0, self.ha), pl.ds(self.ha, self.hb)
        ty, tx, s = self.xor(4), self.xor(2), self.s
        self.y = [self.go(self.acc.at[2 + e, :, ha], self.ry.at[e], (ty, s)) for e in (0, 1)]
        self.x = [self.go(self.acc.at[1 + 2 * e, :, hb], self.rx.at[e], (tx, s)) for e in (0, 1)]

    def add(self, e, lo, size, got):
        def body(j, _):
            own = self.acc[e, j, lo : lo + size, :].astype(F32)
            self.acc[e, j, lo : lo + size, :] = (own + got(j).astype(F32)).astype(BF)
            return 0

        lax.fori_loop(0, 4, body, 0)

    def two(self):
        ha, hb = pl.ds(0, self.ha), pl.ds(self.ha, self.hb)
        ty, tx, s = self.xor(4), self.xor(2), self.s
        self.y[1].wait_recv()
        self.add(1, 0, self.ha, lambda j: self.ry[1, j, :, :])
        self.x2 = self.go(self.acc.at[1, :, ha], self.rx2, (tx, s))
        self.x[1].wait_recv()
        self.add(2, self.ha, self.hb, lambda j: self.rx[1, j, :, :])
        self.y2 = self.go(self.acc.at[2, :, hb], self.ry2, (ty, s))
        self.y[0].wait_recv()
        self.add(0, 0, self.ha, lambda j: self.ry[0, j, :, :])
        self.x[0].wait_recv()
        self.add(0, self.ha, self.hb, lambda j: self.rx[0, j, :, :])

    def three(self):
        self.x2.wait_recv()
        self.add(0, 0, self.ha, lambda j: self.rx2[j, :, :])
        self.y2.wait_recv()
        self.add(0, self.ha, self.hb, lambda j: self.ry2[j, :, :])
        t, s = self.t, self.s
        self.z = [self.go(self.acc.at[0, (s + k) % 4], self.rz.at[k - 1], (t, (s + k) % 4)) for k in (1, 2, 3)]

    def result(self):
        for copy in self.z:
            copy.wait_recv()
        total = self.acc[0, self.s, :, :].astype(F32)
        for k in range(3):
            total = total + self.rz[k, :, :].astype(F32)
        return total

    def drain(self):
        for copy in self.copies:
            copy.wait_send()


def to_shard(first, main, fl, d, out_ref):
    q, p = d // 8, d % 8
    rows = main.shape[0]
    total = out_ref.shape[0]
    fl[4 + 4 * rows : total + 8, :] = jnp.zeros((total + 4 - 4 * rows, 128), F32)
    for b in range(4):
        fl[b : b + 1, :] = first[:, 128 * b : 128 * b + 128]
        fl[pl.ds(4 + b, rows, stride=4), :] = main[:, 128 * b : 128 * b + 128]
    turn = (128 - 16 * p) % 128
    lane = lax.broadcasted_iota(jnp.int32, (total, 128), 1)
    low = pltpu.roll(fl[pl.ds(q, total), :], turn, 1)
    high = pltpu.roll(fl[pl.ds(q + 1, total), :], turn, 1)
    out_ref[...] = jnp.where(lane < 128 - 16 * p, low, high)


def last_rows(part, bound, kind, gain_row):
    rows = part.shape[1]
    at = lax.broadcasted_iota(jnp.int32, (16, D), 0) == kind

    def body(i, _):
        prev = jnp.maximum(i - 1, 0)
        row = part[prev, rows - 16 : rows, :].astype(F32)[15:16, :]
        row = jnp.where(i > 0, row, gain_row)
        bound[i, :, :] = jnp.where(at, row, bound[i, :, :].astype(F32)).astype(BF)
        return 0

    lax.fori_loop(0, 32, body, 0)


def backward_heads(h, qkv, do, live, dqkv, kt, dkv):
    left = halves()
    one, two = jnp.where(left, 1.0, 0.0).astype(BF), jnp.where(left, 0.0, 1.0).astype(BF)
    cols = pl.ds(mult(h * 128, 128), 128)
    kt[...] = jnp.transpose(qkv[1, :, cols].astype(F32)).astype(BF)
    top_lane = lax.broadcasted_iota(jnp.int32, (128, 128), 0) < 64

    def chunk(c, _):
        rows = pl.ds(mult(c * 128, 128), 128)
        q = qkv[0, rows, cols] * jnp.asarray(0.125, BF)
        qm = jnp.concatenate([q * one, q * two], 0)
        g = do[c, :, :, cols].reshape(128, 128)
        gm = jnp.concatenate([g * one, g * two], 0)
        scores = jnp.where(live, nt(qkv[1, :, cols], qm), NEG)
        e = jnp.exp(scores - jnp.max(scores, 0, keepdims=True))
        prob = e * (1.0 / jnp.sum(e, 0, keepdims=True))
        pg = nt(qkv[2, :, cols], gm)
        inner = jnp.sum(prob * pg, 0, keepdims=True)
        sg = (prob * (pg - inner)).astype(BF)
        dk = nn(sg, qm)
        dv = nn(prob.astype(BF), gm)
        dqt = nn(kt[...], sg)
        dq = jnp.transpose(jnp.where(top_lane, dqt[:, 0:128], dqt[:, 128:256])) * 0.125
        dqkv[0, rows, cols] = dq.astype(BF)

        @pl.when(c == 0)
        def _():
            dkv[0] = dk
            dkv[1] = dv

        @pl.when(c > 0)
        def _():
            dkv[0] += dk
            dkv[1] += dv

        return 0

    lax.fori_loop(0, 4, chunk, 0)
    dqkv[1, :, cols] = dkv[0].astype(BF)
    dqkv[2, :, cols] = dkv[1].astype(BF)


def kernel_c(
    cnt, do1, qkv, a1, cf, w1, gains, grad1, p1o, p2, p3, dgain,
    m1, f1, s1, m2, f2, s2, m3, f3, s3,
    cgrad, sh1, sh2, sh3, total,
    do, dqkv, kt, dkv, at, wide, p1, pb, dhs, dhr, fl,
    r1a, aa, rya, rxa, rya2, rxa2, rza,
    r1b, ab, ryb, rxb, ryb2, rxb2, rzb,
    r1c, ac, ryc, rxc, ryc2, rxc2, rzc,
    r1d, ad, ryd, rxd, ryd2, rxd2, rzd,
    ssem, rsem, dss, dsr, hss, hsr, sums, got, zs, nss, nsr,
):
    t, s = here()
    d = 4 * t + s
    barrier = enter(t, s)
    do[s] = do1[:, s, :, :]
    pb[...] = jnp.zeros((32, 16, D), BF)
    sa = Scatter(p1, r1a, aa, rya, rxa, rya2, rxa2, rza, 32, ssem.at[0], rsem.at[0], t, s)
    sb = Scatter(p2, r1b, ab, ryb, rxb, ryb2, rxb2, rzb, 32, ssem.at[1], rsem.at[1], t, s)
    sc = Scatter(p3, r1c, ac, ryc, rxc, ryc2, rxc2, rzc, 64, ssem.at[2], rsem.at[2], t, s)
    pl.semaphore_wait(barrier, 6)
    moves = [
        send(do1.at[:, (s + k) % 4], do.at[s], dss.at[k - 1], dsr.at[k - 1], (t, (s + k) % 4)) for k in (1, 2, 3)
    ]
    sc.core()
    sb.core()
    sc.core_sum()
    sc.one()
    at[...] = jnp.transpose(a1[...].astype(F32)).astype(BF)
    sb.core_sum()
    for copy in moves:
        copy.wait_recv()
    live = lax.broadcasted_iota(jnp.int32, (512, 1), 0) < cnt[0]

    def heads(lo, hi):
        def body(h, _):
            backward_heads(h, qkv, do, live, dqkv, kt, dkv)
            return 0

        lax.fori_loop(lo, hi, body, 0)

    heads(0, 2)
    sc.two()
    sb.one()
    heads(2, 3)
    sc.three()
    heads(3, 4)
    sb.two()
    gain = gains[0:1, :]
    dg = jnp.zeros((1, D), F32)

    def norm_back(i, dg):
        rows = pl.ds(mult(i * 128, 128), 128)
        da = nt(dqkv[0, rows, :], w1[0]) + nt(dqkv[1, rows, :], w1[1]) + nt(dqkv[2, rows, :], w1[2])
        h = cf[i].astype(F32).reshape(128, D)
        x = h - jnp.mean(h, 1, keepdims=True)
        rstd = lax.rsqrt(jnp.mean(x * x, 1, keepdims=True) + 1e-5)
        x = x * rstd
        dg = dg + jnp.sum(da * x, 0, keepdims=True)
        dx = da * gain
        dh = rstd * (dx - jnp.mean(dx, 1, keepdims=True) - x * jnp.mean(dx * x, 1, keepdims=True))
        dhs[i] = dh.astype(BF).reshape(4, 32, D)
        return dg

    dg = lax.fori_loop(0, 4, norm_back, dg)

    def weights(i, _):
        j, r = i // 4, i % 4
        part = nn(at[pl.ds(mult(r * 128, 128), 128), :], dqkv[j])
        for b in range(4):
            wide[b, pl.ds(384 * r + j, 128, stride=3), :] = part[:, 128 * b : 128 * b + 128]
        return 0

    lax.fori_loop(0, 12, weights, 0)

    def narrow(i, _):
        rows = pl.ds(mult(i * 64, 64), 64)
        for b in range(4):
            p1[i, :, 128 * b : 128 * b + 128] = wide[b, rows, :].astype(BF)
        return 0

    lax.fori_loop(0, 24, narrow, 0)

    def copy_out(i, _):
        p1[24 + i] = p1o[pl.ds(mult(i * 64, 64), 64), :]
        return 0

    lax.fori_loop(0, 8, copy_out, 0)
    last_rows(p1, pb, 0, dg)
    last_rows(p2, pb, 1, dgain[1:2, :])
    last_rows(p3, pb, 2, dgain[2:3, :])
    sd = Scatter(pb, r1d, ad, ryd, rxd, ryd2, rxd2, rzd, 0, ssem.at[3], rsem.at[3], t, s)
    sd.ha, sd.hb = 16, 16
    sa.core()
    sd.core()
    homes = [
        send(dhs.at[(s + k) % 4], dhr.at[:, s], hss.at[k - 1], hsr.at[k - 1], (t, (s + k) % 4)) for k in (1, 2, 3)
    ]
    sb.three()
    sa.core_sum()
    sa.one()
    sd.core_sum()
    bound_one(sd)
    main3 = sc.result()
    main2 = sb.result()
    sa.two()
    bound_two(sd)
    sa.three()
    bound_three(sd)
    cgrad[:, s, :, :] = grad1[:, s, :, :] + dhs[s].astype(F32)
    for k in (1, 2, 3):
        homes[k - 1].wait_recv()
        f = (s + 4 - k) % 4
        cgrad[:, f, :, :] = grad1[:, f, :, :] + dhr[:, f, :, :].astype(F32)
    main1 = sa.result()
    first = sd.result()
    to_shard(first[0:1, :], main1, fl, d, sh1)
    to_shard(first[1:2, :], main2, fl, d, sh2)
    to_shard(first[2:3, :], main3, fl, d, sh3)
    sums[0] = jnp.zeros((32, 128), F32)
    squares(sh1, m1, f1, s1, sums.at[0], d, 3 * D, 0)
    squares(sh2, m2, f2, s2, sums.at[0], d, 3 * D, 1)
    squares(sh3, m3, f3, s3, sums.at[0], d, 4 * D, 2)
    total[...], adds = sum_all(sums, got, zs, nss, nsr, t, s)
    for one in (sa, sb, sc, sd):
        one.drain()
    for copy in moves + homes + adds:
        copy.wait_send()


def bound_one(sd):
    sd.y = [sd.go(sd.acc.at[2 + e], sd.ry.at[e], (sd.xor(4), sd.s)) for e in (0, 1)]


def bound_two(sd):
    for e in (1, 0):
        sd.y[e].wait_recv()
        sd.add(e, 0, 16, lambda j, e=e: sd.ry[e, j, :, :])
        if e:
            sd.x2 = sd.go(sd.acc.at[1], sd.rx2, (sd.xor(2), sd.s))


def bound_three(sd):
    sd.x2.wait_recv()
    sd.add(0, 0, 16, lambda j: sd.rx2[j, :, :])
    t, s = sd.t, sd.s
    sd.z = [sd.go(sd.acc.at[0, (s + k) % 4], sd.rz.at[k - 1], (t, (s + k) % 4)) for k in (1, 2, 3)]


def scatter_scratch(rows, ha, hb):
    return [
        pltpu.VMEM((4, 4, rows, D), BF), pltpu.VMEM((4, 4, rows, D), BF),
        pltpu.VMEM((2, 4, ha, D), BF), pltpu.VMEM((2, 4, hb, D), BF),
        pltpu.VMEM((4, hb, D), BF), pltpu.VMEM((4, ha, D), BF), pltpu.VMEM((3, rows, D), BF),
    ]


def call_c(cnt, do1, qkv, a1, cf, w1, gains, grad1, p1o, p2, p3, dgain, params):
    sds = jax.ShapeDtypeStruct
    vm = pl.BlockSpec(memory_space=pltpu.VMEM)
    return pl.pallas_call(
        kernel_c,
        name="kernel_c",
        out_shape=(sds((4, 4, 32, D), F32), sds((264, 128), F32), sds((264, 128), F32), sds((520, 128), F32), sds((32, 128), F32)),
        in_specs=[pl.BlockSpec(memory_space=pltpu.SMEM)] + [vm] * 20,
        out_specs=(vm,) * 5,
        scratch_shapes=[
            pltpu.VMEM((4, 4, 32, D), BF), pltpu.VMEM((3, D, D), BF), pltpu.VMEM((128, D), BF),
            pltpu.VMEM((2, D, 128), F32), pltpu.VMEM((D, D), BF), pltpu.VMEM((4, 3 * D, 128), F32),
            pltpu.VMEM((32, 64, D), BF), pltpu.VMEM((32, 16, D), BF),
            pltpu.VMEM((4, 4, 32, D), BF), pltpu.VMEM((4, 4, 32, D), BF), pltpu.VMEM((528, 128), F32),
            *scatter_scratch(64, 32, 32), *scatter_scratch(64, 32, 32), *scatter_scratch(128, 64, 64),
            *scatter_scratch(16, 16, 16),
            pltpu.SemaphoreType.DMA((4, 14)), pltpu.SemaphoreType.DMA((4, 14)),
            pltpu.SemaphoreType.DMA((3,)), pltpu.SemaphoreType.DMA((3,)),
            pltpu.SemaphoreType.DMA((3,)), pltpu.SemaphoreType.DMA((3,)),
            pltpu.VMEM((3, 32, 128), F32), pltpu.VMEM((3, 32, 128), F32), pltpu.VMEM((4, 32, 128), F32),
            pltpu.SemaphoreType.DMA((6,)), pltpu.SemaphoreType.DMA((6,)),
        ],
        compiler_params=pltpu.CompilerParams(collective_id=2, has_side_effects=True, vmem_limit_bytes=60 << 20),
    )(cnt, do1, qkv, a1, cf, w1, gains, grad1, p1o, p2, p3, dgain, *params)


def turn(x):
    return jnp.transpose(x)


def stats(h):
    x = h - jnp.mean(h, 1, keepdims=True)
    rstd = lax.rsqrt(jnp.mean(x * x, 1, keepdims=True) + 1e-5)
    return x * rstd, rstd


def norm_grad(h, da, gain):
    x, rstd = stats(h)
    dgain = jnp.sum(da * x, 0, keepdims=True)
    dx = da * gain
    dh = rstd * (dx - jnp.mean(dx, 1, keepdims=True) - x * jnp.mean(dx * x, 1, keepdims=True))
    return dh, dgain


def block(g):
    return pl.ds(mult(g * 128, 128), 128)


def feature_mask(fcnt, axis):
    shape = (256, 128) if axis else (128, 256)
    query = lax.broadcasted_iota(jnp.int32, shape, 1 - axis)
    key = lax.broadcasted_iota(jnp.int32, shape, axis)
    return (query % 32 == key % 32) & (key // 32 < fcnt)


def feature_forward(qkv, o2, fcnt):
    left = halves()
    one = jnp.where(left, 0.125, 0.0).astype(BF)
    two = jnp.where(left, 0.0, 0.125).astype(BF)
    ok = feature_mask(fcnt, 1)

    def body(n, _):
        rows, cols = block(n // 4), block(n % 4)
        q = qkv[0, rows, cols]
        qm = jnp.concatenate([q * one, q * two], 0)
        scores = jnp.where(ok, nt(qm, qkv[1, rows, cols]), NEG)
        e = jnp.exp(scores - jnp.max(scores, 1, keepdims=True))
        prob = (e * (1.0 / jnp.sum(e, 1, keepdims=True))).astype(BF)
        o = nn(prob, qkv[2, rows, cols])
        o2[rows, cols] = jnp.where(left, o[0:128], o[128:256]).astype(BF)
        return 0

    lax.fori_loop(0, 16, body, 0)


def feature_backward(qkv, do, dqkv, fcnt):
    left = halves()
    one, two = jnp.where(left, 1.0, 0.0).astype(BF), jnp.where(left, 0.0, 1.0).astype(BF)
    ok = feature_mask(fcnt, 0)
    top_lane = lax.broadcasted_iota(jnp.int32, (128, 128), 0) < 64

    def body(n, _):
        rows, cols = block(n // 4), block(n % 4)
        q = qkv[0, rows, cols] * jnp.asarray(0.125, BF)
        qm = jnp.concatenate([q * one, q * two], 0)
        g = do[rows, cols]
        gm = jnp.concatenate([g * one, g * two], 0)
        k = qkv[1, rows, cols]
        scores = jnp.where(ok, nt(k, qm), NEG)
        e = jnp.exp(scores - jnp.max(scores, 0, keepdims=True))
        prob = e * (1.0 / jnp.sum(e, 0, keepdims=True))
        pg = nt(qkv[2, rows, cols], gm)
        sg = (prob * (pg - jnp.sum(prob * pg, 0, keepdims=True))).astype(BF)
        dqt = nn(turn(k), sg)
        dq = turn(jnp.where(top_lane, dqt[:, 0:128], dqt[:, 128:256])) * 0.125
        dqkv[0, rows, cols] = dq.astype(BF)
        dqkv[1, rows, cols] = nn(sg, qm).astype(BF)
        dqkv[2, rows, cols] = nn(prob.astype(BF), gm).astype(BF)
        return 0

    lax.fori_loop(0, 16, body, 0)


def four_blocks(body, init=0):
    return lax.fori_loop(0, 4, body, init)


def flat(x):
    return x.reshape(128, D)


def cube(x):
    return x.reshape(4, 32, D)


def narrow_to(wide, part, slots, rows):
    def body(i, _):
        at = pl.ds(mult(i * rows, rows), rows)
        for b in range(4):
            part[i, :, 128 * b : 128 * b + 128] = wide[b, at, :].astype(BF)
        return 0

    lax.fori_loop(0, slots, body, 0)


def store_wide(wide, j, ways, value):
    for b in range(4):
        wide[b, pl.ds(j, value.shape[0], stride=ways), :] = value[:, 128 * b : 128 * b + 128]


def mlp(a3, a3t, g, h2, wup, wdn, h3, da, zb, dub, u, dz, wide, p3):
    h3[...] = h2[...]
    da[...] = jnp.zeros((512, D), F32)

    def body(j, _):
        u[...] = nn(a3[...], wup[j])
        dz[...] = nt(g[...], wdn[j]).astype(BF)

        def act(r, _):
            rows = pl.ds(mult(r * 64, 64), 64)
            x = u[rows, :]
            cdf = 0.5 * (1.0 + lax.erf(x * 0.7071067811865476))
            zb[rows, :] = (x * cdf).astype(BF)
            slope = cdf + x * (0.3989422804014327 * jnp.exp(-0.5 * x * x))
            dub[rows, :] = (slope * dz[rows, :].astype(F32)).astype(BF)
            return 0

        lax.fori_loop(0, 8, act, 0)
        h3[...] += nn(zb[...], wdn[j])
        da[...] += nt(dub[...], wup[j])
        store_wide(wide, j, 4, nn(a3t[...], dub[...]))
        dw = nn(turn(zb[...]), g[...]).astype(BF)
        for i in range(4):
            p3[16 + 4 * j + i] = dw[128 * i : 128 * i + 128]
        return 0

    lax.fori_loop(0, 4, body, 0)
    narrow_to(wide, p3, 16, 128)


def middle_forward(s, cells, top, o1, wo1, w2, wo2, gains, scnt, fcnt, h1, h2, a2, qkv, o2, a3, g):
    gain2, gain3 = gains[1:2, :], gains[2:3, :]
    h1[...] = nn(o1[...].reshape(512, D), wo1[...])

    def first(r, _):
        rows = block(r)
        h = h1[rows, :] + flat(cells[r].astype(F32))
        h1[rows, :] = h
        x, _ = stats(h)
        a2[rows, :] = (x * gain2).astype(BF)
        n = lax.broadcasted_iota(jnp.int32, (128, 1), 0)
        live = (n // 32 < fcnt) & (128 * s + 32 * r + n % 32 < scnt)
        g[rows, :] = jnp.where(live, flat(top[r].astype(F32)), 0.0).astype(BF)
        return 0

    four_blocks(first)

    def project(j, _):
        qkv[j] = nn(a2[...], w2[j]).astype(BF)
        return 0

    lax.fori_loop(0, 3, project, 0)
    feature_forward(qkv, o2, fcnt)
    h2[...] = h1[...] + nn(o2[...], wo2[...])

    def second(r, _):
        rows = block(r)
        x, _ = stats(h2[rows, :])
        a3[rows, :] = (x * gain3).astype(BF)
        return 0

    four_blocks(second)


def layer_output(s, h3, lout, scnt, fcnt):
    def last(r, _):
        n = lax.broadcasted_iota(jnp.int32, (128, 1), 0)
        live = (n // 32 < fcnt) & (128 * s + 32 * r + n % 32 < scnt)
        lout[r] = cube(jnp.where(live, h3[block(r), :], 0.0).astype(BF))
        return 0

    four_blocks(last)


def feature_grads(o1, wo1, w2, wo2, gains, fcnt, h1, h2, a2, qkv, o2, g, da, b, do, dqkv, wide, p2, dwo1, do1, gr, dgain):
    gain2, gain3 = gains[1:2, :], gains[2:3, :]

    def third(r, dg):
        rows = block(r)
        dh, part = norm_grad(h2[rows, :], da[rows, :], gain3)
        total = g[rows, :].astype(F32) + dh
        gr[r] = cube(total)
        b[rows, :] = total.astype(BF)
        return dg + part

    dg3 = four_blocks(third, jnp.zeros((1, D), F32))
    do[...] = nt(b[...], wo2[...]).astype(BF)
    dw = nn(turn(o2[...]), b[...]).astype(BF)
    for i in range(8):
        p2[24 + i] = dw[64 * i : 64 * i + 64]
    feature_backward(qkv, do, dqkv, fcnt)

    def weights(j, _):
        store_wide(wide, j, 3, nn(turn(a2[...]), dqkv[j]))
        return 0

    lax.fori_loop(0, 3, weights, 0)
    narrow_to(wide, p2, 24, 64)
    da[...] = nt(dqkv[0], w2[0]) + nt(dqkv[1], w2[1]) + nt(dqkv[2], w2[2])

    def fourth(r, dg):
        rows = block(r)
        dh, part = norm_grad(h1[rows, :], da[rows, :], gain2)
        total = flat(gr[r]) + dh
        gr[r] = cube(total)
        b[rows, :] = total.astype(BF)
        return dg + part

    dg2 = four_blocks(fourth, jnp.zeros((1, D), F32))
    do1[...] = nt(b[...], wo1[...]).astype(BF).reshape(4, 4, 32, D)
    dwo1[...] = nn(turn(o1[...].reshape(512, D)), b[...]).astype(BF)
    n = lax.broadcasted_iota(jnp.int32, (8, D), 0)
    dgain[...] = jnp.where(n == 1, dg2, jnp.where(n == 2, dg3, 0.0))


def kernel_b(
    scnt, fcnt, cells, top, o1, wo1, w2, wo2, wup, wdn, gains,
    lout, gr, do1, dwo1, p2, p3, dgain,
    h1, h2, a2, qkv, o2, a3, a3t, g, h3, da, zb, dub, u, dz, wide, b, do, dqkv,
):
    s = lax.axis_index("samp")
    middle_forward(s, cells, top, o1, wo1, w2, wo2, gains, scnt[0], fcnt[0], h1, h2, a2, qkv, o2, a3, g)
    a3t[...] = turn(a3[...])
    mlp(a3, a3t, g, h2, wup, wdn, h3, da, zb, dub, u, dz, wide, p3)
    layer_output(s, h3, lout, scnt[0], fcnt[0])
    feature_grads(
        o1, wo1, w2, wo2, gains, fcnt[0], h1, h2, a2, qkv, o2, g, da, b, do, dqkv, wide, p2, dwo1, do1, gr, dgain
    )


def middle_scratch():
    w = pltpu.VMEM((D, D), F32)
    n = pltpu.VMEM((D, D), BF)
    three = pltpu.VMEM((3, D, D), BF)
    return [w, w, n, three, n, n, n, n, w, w, n, n, w, n, pltpu.VMEM((4, 4 * D, 128), F32), n, n, three]


def call_b(scnt, fcnt, cells, top, o1, wo1, w2, wo2, wup, wdn, gains):
    sds = jax.ShapeDtypeStruct
    vm = pl.BlockSpec(memory_space=pltpu.VMEM)
    sm = pl.BlockSpec(memory_space=pltpu.SMEM)
    return pl.pallas_call(
        kernel_b,
        name="kernel_b",
        out_shape=(
            sds((4, 4, 32, D), BF), sds((4, 4, 32, D), F32), sds((4, 4, 32, D), BF), sds((D, D), BF),
            sds((32, 64, D), BF), sds((32, 128, D), BF), sds((8, D), F32),
        ),
        in_specs=[sm, sm] + [vm] * 9,
        out_specs=(vm,) * 7,
        scratch_shapes=middle_scratch(),
        compiler_params=pltpu.CompilerParams(vmem_limit_bytes=60 << 20),
    )(scnt, fcnt, cells, top, o1, wo1, w2, wo2, wup, wdn.reshape(4, D, D), gains)


def local(x):
    return jnp.transpose(x.reshape(4, 32, 4, D), (0, 2, 1, 3))


def globe(x):
    return jnp.transpose(x, (0, 2, 1, 3)).reshape(1, 128, 4, D)


def fast_device(cells, out_grad, scnt, fcnt, b1, f1, s1, b2, f2, s2, b3, f3, s3):
    here_cells, top = local(cells), local(out_grad)
    o1, w1, wo1, w2, wo2, wup, wdn, gains, qkv, a1, cf = call_a(scnt, here_cells, b1, b2, b3)
    out, gr, do1, dwo1, p2, p3, dgain = call_b(scnt, fcnt, here_cells, top, o1, wo1, w2, wo2, wup, wdn, gains)
    params = (b1, f1, s1, b2, f2, s2, b3, f3, s3)
    cgrad, sh1, sh2, sh3, total = call_c(scnt, do1, qkv, a1, cf, w1, gains, gr, dwo1, p2, p3, dgain, params)
    outs = call_e(total, (sh1, sh2, sh3), params)
    return (globe(out), globe(cgrad), *outs)


def step(*args):
    cells = args[0]
    fits = lax.axis_size("task") == 8 and lax.axis_size("samp") == 4 and cells.shape == (1, 128, 4, D)
    return fast_device(*args) if fits else on_device(*args)


def solution(mesh):
    placed = (
        P("task", "samp", None, None),
        P("task", "samp", None, None),
        P("task"),
        P("task"),
        P(("task", "samp")),
        P(("task", "samp")),
        P(("task", "samp")),
        P(("task", "samp")),
        P(("task", "samp")),
        P(("task", "samp")),
        P(("task", "samp")),
        P(("task", "samp")),
        P(("task", "samp")),
    )
    return jax.shard_map(
        step,
        mesh=mesh,
        in_specs=placed,
        out_specs=(
            P("task", "samp", None, None),
            P("task", "samp", None, None),
            P(("task", "samp")),
            P(("task", "samp")),
            P(("task", "samp")),
            P(("task", "samp")),
            P(("task", "samp")),
            P(("task", "samp")),
            P(("task", "samp")),
            P(("task", "samp")),
            P(("task", "samp")),
            P(("task", "samp")),
            P(("task", "samp")),
            P(("task", "samp")),
            P(("task", "samp")),
            P(("task", "samp")),
            P(("task", "samp")),
            P(),
        ),
        check_vma=False,
    )
```

profile of v0, /device:TPU:0, one launch (start us, length us, event | category | flops | bytes accessed | tf_op | source)
XLA Modules:
  0.0 226.0 jit_solution(6899755883927585418)
XLA Ops:
  1.9 2.4 %copy_bitcast_fusion = (bf16[4,4,32,512]{3,2,1,0:T(8,128)(2,1)}, bf16[4,4,32,512]{3,2,1,0:T(8,128)(2,1)}) fusion(bf16[4,32,4,512]{3,2,1,0:T(4,128)(2,1)} %bitcast.16, bf16[4,32,4,512]{3,2,1,0:T(4,128)(2,1)} %bitcast.17), kind=kLoop, calls=%fused_computation | loop fusion | bytes 2097152 | tf_op jit(solution)/shard_map/transpose | solution.py:1438
  4.4 70.4 %kernel_a.1 = (bf16[4,4,32,512]{3,2,1,0:T(8,128)(2,1)}, bf16[3,512,512]{2,1,0:T(8,128)(2,1)}, bf16[512,512]{1,0:T(8,128)(2,1)}, bf16[3,512,512]{2,1,0:T(8,128)(2...) custom-call(s32[1]{0:T(128)S(6)} %copy.47.cnt.scnt, ...), custom_call_target="tpu_custom_call" | custom-call | tf_op jit(solution)/shard_map/kernel_a/pallas_call | solution.py:684
  74.8 43.7 %kernel_b.1 = (bf16[4,4,32,512]{3,2,1,0:T(8,128)(2,1)}, f32[4,4,32,512]{3,2,1,0:T(8,128)}, bf16[4,4,32,512]{3,2,1,0:T(8,128)(2,1)}, bf16[512,512]{1,0:T(8,128)(2...) custom-call(s32[1]{0:T(128)S(6)} %copy.47.cnt.scnt, s32[1]{0:T(128)S(6)} %copy.48.fcnt, ...), custom_call_target="tpu_custom_call" | custom-call | tf_op jit(solution)/shard_map/kernel_b/pallas_call | solution.py:1423
  118.5 97.6 %kernel_c.1 = (f32[4,4,32,512]{3,2,1,0:T(8,128)}, f32[264,128]{1,0:T(8,128)}, f32[264,128]{1,0:T(8,128)}, f32[520,128]{1,0:T(8,128)}, f32[32,128]{1,0:T(8,128)}) custom-call(s32[1]{0:T(128)S(6)} %copy.47.cnt.scnt, bf16[4,4,32,512]{3,2,1,0:T(8,128)(2,1)} %get-tuple-element.65.do1, bf16[3,512,512]{2,1,0:T(8,128)(2,1)} %get-tuple-element.66.qkv, ...), custom_call_target="tpu_custom_call" | custom-call | tf_op jit(solution)/shard_map/kernel_c/pallas_call | solution.py:1155
  216.1 0.0 copy-start.13
  216.1 0.0 copy-done.14
  216.2 1.2 copy.38
  217.4 0.0 copy-done.13
  217.4 0.0 copy-start.3
  217.4 0.0 copy-start.4
  217.4 0.0 copy-start.5
  217.4 0.0 copy-start.6
  217.4 0.0 copy-start.7
  217.5 0.0 copy-start.8
  217.5 0.0 copy-start.9
  217.5 0.0 copy-start.10
  217.5 0.0 copy-start.11
  217.5 0.0 copy-start.12
  217.5 0.1 copy.37
  217.6 1.6 copy.39
  219.3 0.0 copy-done
  219.3 0.0 copy-done.2
  219.4 6.0 %kernel_e.1 = (f32[32784]{0:T(1024)}, f32[32784]{0:T(1024)}, f32[32784]{0:T(1024)}, f32[32784]{0:T(1024)}, bf16[32784]{0:T(1024)(128)(2,1)}, /*index=5*/f32[3278...) custom-call(f32[32,128]{1,0:T(8,128)S(1)} %copy-done.12, ...), custom_call_target="tpu_custom_call" | custom-call | tf_op jit(solution)/shard_map/kernel_e/pallas_call | solution.py:827
  225.3 0.6 copy.40
  (16 shorter events, 0.1 us)
Async XLA Ops:
  118.5 97.6 %copy-start.14 = (bf16[4,4,32,512]{3,2,1,0:T(8,128)(2,1)S(1)}, bf16[4,4,32,512]{3,2,1,0:T(8,128)(2,1)}, u32[]{:S(2)}) copy-start(bf16[4,4,32,512]{3,2,1,0:T(8,128)(2,1)} %get-tuple-element.64) | copy-start | bytes 1572868
  216.1 1.3 copy-start.13
  217.4 1.9 copy-start
  217.4 1.9 copy-start.1
  217.4 1.9 copy-start.2
  217.4 1.9 copy-start.3
  217.4 1.9 copy-start.4
  217.4 1.9 copy-start.5
  217.4 1.9 copy-start.6
  217.4 1.9 copy-start.7
  217.5 1.9 copy-start.8
  217.5 1.9 copy-start.9
  217.5 1.9 copy-start.10
  217.5 1.9 copy-start.11
  217.5 1.9 copy-start.12
where the time goes:
time: 226 us
  Pallas kernels  218 us (96%)
  local copies, waits for them, and re-layouts  6.13 us (3%)
    pallas_call x1, Pallas kernels, call_c(): pl.pallas_call(kernel_c, name='kernel_c', out_shape=(sds((4, 4, 32, D), F...  97.6 us
    pallas_call x1, Pallas kernels, call_a(): pl.pallas_call(kernel_a, name='kernel_a', out_shape=(sds((4, 4, 32, D), B...  70.4 us
    pallas_call x1, Pallas kernels, call_b(): pl.pallas_call(kernel_b, name='kernel_b', out_shape=(sds((4, 4, 32, D), B...  43.7 us
    pallas_call x1, Pallas kernels, call_e(): pl.pallas_call(kernel_e, name='kernel_e', out_shape=(*shapes, sds((9, 2),...  5.96 us

commit v1 on v0

--- a/solution.py
+++ b/solution.py
@@ -1434,6 +1434,395 @@
     )(scnt, fcnt, cells, top, o1, wo1, w2, wo2, wup, wdn.reshape(4, D, D), gains)
 
 
+class Reduce:
+    def __init__(self, part, r1, ry, rx, ry2, rx2, rz, half, ssem, rsem, t, s):
+        self.part, self.r1 = part, r1
+        self.ry, self.rx, self.ry2, self.rx2, self.rz = ry, rx, ry2, rx2, rz
+        self.rows = part.shape[1]
+        self.half = half
+        self.ssem, self.rsem, self.t, self.s = ssem, rsem, t, s
+        self.count = 0
+        self.copies = []
+
+    def go(self, src, dst, peer):
+        i = self.count
+        self.count += 1
+        copy = send(src, dst, self.ssem.at[i], self.rsem.at[i], peer)
+        self.copies.append(copy)
+        return copy
+
+    def xor(self, e):
+        return jnp.bitwise_xor(self.t, e)
+
+    def group(self, e, rows=None):
+        slots = pl.ds(4 * self.xor(2 * e), 4)
+        return self.part.at[slots] if rows is None else self.part.at[slots, rows]
+
+    def core(self):
+        tc = self.xor(1)
+        self.c = [
+            self.go(self.part.at[pl.ds(4 * jnp.bitwise_xor(tc, 2 * e), 4)], self.r1.at[e], (tc, self.s))
+            for e in (2, 3, 1, 0)
+        ]
+
+    def add(self, e, lo, size, got):
+        base = 4 * self.xor(2 * e)
+
+        def body(j, _):
+            own = self.part[base + j, lo : lo + size, :].astype(F32)
+            self.part[base + j, lo : lo + size, :] = (own + got(j).astype(F32)).astype(BF)
+            return 0
+
+        lax.fori_loop(0, 4, body, 0)
+
+    def one(self):
+        ha, hb = pl.ds(0, self.half), pl.ds(self.half, self.rows - self.half)
+        ty, tx, s = self.xor(4), self.xor(2), self.s
+        self.y, self.x = {}, {}
+        for n, e in enumerate((2, 3, 1, 0)):
+            self.c[n].wait_recv()
+            self.add(e, 0, self.rows, lambda j, e=e: self.r1[e, j, :, :])
+            if e in (2, 3):
+                self.y[e - 2] = self.go(self.group(e, ha), self.ry.at[e - 2], (ty, s))
+            if e in (3, 1):
+                self.x[e // 2] = self.go(self.group(e, hb), self.rx.at[e // 2], (tx, s))
+
+    def two(self):
+        a, b = self.half, self.rows - self.half
+        ha, hb = pl.ds(0, a), pl.ds(a, b)
+        ty, tx, s = self.xor(4), self.xor(2), self.s
+        self.y[1].wait_recv()
+        self.add(1, 0, a, lambda j: self.ry[1, j, :, :])
+        self.x2 = self.go(self.group(1, ha), self.rx2, (tx, s))
+        self.x[1].wait_recv()
+        self.add(2, a, b, lambda j: self.rx[1, j, :, :])
+        self.y2 = self.go(self.group(2, hb), self.ry2, (ty, s))
+        self.y[0].wait_recv()
+        self.add(0, 0, a, lambda j: self.ry[0, j, :, :])
+        self.x[0].wait_recv()
+        self.add(0, a, b, lambda j: self.rx[0, j, :, :])
+
+    def three(self):
+        a, b = self.half, self.rows - self.half
+        self.x2.wait_recv()
+        self.add(0, 0, a, lambda j: self.rx2[j, :, :])
+        self.y2.wait_recv()
+        self.add(0, a, b, lambda j: self.ry2[j, :, :])
+        t, s = self.t, self.s
+        self.z = [
+            self.go(self.part.at[4 * t + (s + k) % 4], self.rz.at[k - 1], (t, (s + k) % 4)) for k in (1, 2, 3)
+        ]
+
+    def result(self):
+        for copy in self.z:
+            copy.wait_recv()
+        total = self.part[4 * self.t + self.s, :, :].astype(F32)
+        for k in range(3):
+            total = total + self.rz[k, :, :].astype(F32)
+        return total
+
+    def drain(self):
+        for copy in self.copies:
+            copy.wait_send()
+
+
+def edge_rows(part, bound, kind):
+    rows = min(128, part.shape[1])
+    end = 64 if rows == 80 else rows
+    at = lax.broadcasted_iota(jnp.int32, (16, D), 0) == kind
+
+    def body(i, _):
+        row = part[i - 1, end - 16 : end, :].astype(F32)[15:16, :]
+        bound[i, 64:80, :] = jnp.where(at, row, bound[i, 64:80, :].astype(F32)).astype(BF)
+        return 0
+
+    lax.fori_loop(1, 32, body, 0)
+
+
+def edge_gains(bound, gain1, dgain):
+    n = lax.broadcasted_iota(jnp.int32, (16, D), 0)
+    rows = jnp.where(n == 0, gain1, jnp.where(n == 1, dgain[1:2, :], jnp.where(n == 2, dgain[2:3, :], 0.0)))
+    bound[0, 64:80, :] = rows.astype(BF)
+
+
+def to_rows(main, fl):
+    rows = main.shape[0]
+    for b in range(4):
+        fl[pl.ds(4 + b, rows, stride=4), :] = main[:, 128 * b : 128 * b + 128]
+
+
+def to_shard(first, fl, rows, d, out_ref):
+    q, p = d // 8, d % 8
+    total = out_ref.shape[0]
+    fl[4 + 4 * rows : total + 8, :] = jnp.zeros((total + 4 - 4 * rows, 128), F32)
+    for b in range(4):
+        fl[b : b + 1, :] = first[:, 128 * b : 128 * b + 128]
+    back = (128 - 16 * p) % 128
+    lane = lax.broadcasted_iota(jnp.int32, (total, 128), 1)
+    low = pltpu.roll(fl[pl.ds(q, total), :], back, 1)
+    high = pltpu.roll(fl[pl.ds(q + 1, total), :], back, 1)
+    out_ref[...] = jnp.where(lane < 128 - 16 * p, low, high)
+
+
+class Refs:
+    def __init__(self, names, refs):
+        for name, ref in zip(names, refs, strict=True):
+            setattr(self, name, ref)
+
+
+def reduce_names(n):
+    return [k + n for k in ("r1", "ry", "rx", "ry2", "rx2", "rz")]
+
+
+def reduce_scratch(rows, a):
+    b = rows - a
+    return [
+        pltpu.VMEM((4, 4, rows, D), BF), pltpu.VMEM((2, 4, a, D), BF), pltpu.VMEM((2, 4, b, D), BF),
+        pltpu.VMEM((4, b, D), BF), pltpu.VMEM((4, a, D), BF), pltpu.VMEM((3, rows, D), BF),
+    ]
+
+
+PARAMS = ["m1", "f1", "s1", "m2", "f2", "s2", "m3", "f3", "s3"]
+WIDE = pltpu.VMEM((D, D), F32)
+NARROW = pltpu.VMEM((D, D), BF)
+THREE = pltpu.VMEM((3, D, D), BF)
+FOUR = pltpu.VMEM((4, D, D), BF)
+TILE = pltpu.VMEM((4, 4, 32, D), BF)
+DMA = pltpu.SemaphoreType.DMA
+SCRATCH = {
+    "g1": pltpu.VMEM((32, 80, D), BF), "g2": pltpu.VMEM((32, 64, D), BF), "g3": pltpu.VMEM((32, 128, D), BF),
+    "wide": pltpu.VMEM((4, 4 * D, 128), F32), "sh": pltpu.VMEM((536, 128), F32), "ro": pltpu.VMEM((536, 128), F32),
+    "w1": THREE, "wo1": NARROW, "w2": THREE, "wo2": NARROW, "wup": FOUR, "wdn": FOUR,
+    "gains": pltpu.VMEM((8, D), F32), "dgain": pltpu.VMEM((8, D), F32),
+    "cf": TILE, "a1": NARROW, "qkv1": THREE, "o1c": pltpu.VMEM((3, 4, 32, D), BF), "o1": TILE,
+    "h1": WIDE, "h2": WIDE, "a2": NARROW, "qkv2": THREE, "o2": NARROW, "a3": NARROW, "at": NARROW, "g": NARROW,
+    "h3": WIDE, "da": WIDE, "zb": NARROW, "dub": NARROW, "u": WIDE, "dz": NARROW, "b": NARROW, "do2": NARROW,
+    "dqkv": THREE, "gr": pltpu.VMEM((4, 4, 32, D), F32), "do1": TILE, "do": TILE, "dwo1": NARROW,
+    "kt": pltpu.VMEM((128, D), BF), "dkv": pltpu.VMEM((2, D, 128), F32), "dhs": TILE, "dhr": TILE,
+    **dict(zip(reduce_names("a"), reduce_scratch(80, 32))),
+    **dict(zip(reduce_names("b"), reduce_scratch(64, 32))),
+    **dict(zip(reduce_names("c"), reduce_scratch(128, 64))),
+    "fl1": pltpu.VMEM((272, 128), F32), "fl2": pltpu.VMEM((272, 128), F32), "fl3": pltpu.VMEM((528, 128), F32),
+    "sums": pltpu.VMEM((3, 32, 128), F32), "got": pltpu.VMEM((3, 32, 128), F32), "zs": pltpu.VMEM((4, 32, 128), F32),
+    "gs": DMA((3, 16)), "gq": DMA((3, 16)), "rs": DMA((3, 16)), "rq": DMA((3, 16)),
+    "as1": DMA((3,)), "aq1": DMA((3,)), "as2": DMA((3,)), "aq2": DMA((3,)),
+    "as3": DMA((3,)), "aq3": DMA((3,)), "as4": DMA((3,)), "aq4": DMA((3,)), "ns": DMA((6,)), "nq": DMA((6,)),
+}
+INPUTS = ["scnt", "fcnt", "cells", "top"] + PARAMS
+OUTPUTS = ["lout", "cgrad", "sh1", "sh2", "sh3", "total"]
+
+
+def kernel_m(*refs):
+    r = Refs(INPUTS + OUTPUTS + list(SCRATCH), refs)
+    t, s = here()
+    d = 4 * t + s
+    scnt, fcnt = r.scnt[0], r.fcnt[0]
+    barrier = enter(t, s)
+    ga = Gather(r.g1, 32, r.gs.at[0], r.gq.at[0], t, s)
+    gb = Gather(r.g2, 32, r.gs.at[1], r.gq.at[1], t, s)
+    gc = Gather(r.g3, 64, r.gs.at[2], r.gq.at[2], t, s)
+    first1 = realign(r.m1, r.sh, d, 64, r.g1, d, r.ro)
+    first2 = realign(r.m2, r.sh, d, 64, r.g2, d, r.ro)
+    first3 = realign(r.m3, r.sh, d, 128, r.g3, d, r.ro)
+    row = lax.broadcasted_iota(jnp.int32, (16, D), 0)
+    firsts = jnp.where(row == 0, first1, jnp.where(row == 1, first2, jnp.where(row == 2, first3, 0.0)))
+    r.g1[d, 64:80, :] = firsts.astype(BF)
+    pl.semaphore_wait(barrier, 6)
+    ga.z()
+    r.cf[s] = r.cells[:, s, :, :]
+    moves = [
+        send(r.cells.at[:, (s + k) % 4], r.cf.at[s], r.as1.at[k - 1], r.aq1.at[k - 1], (t, (s + k) % 4))
+        for k in (1, 2, 3)
+    ]
+    ga.one()
+    ga.two()
+    for copy in moves:
+        copy.wait_recv()
+    gb.z()
+    gc.z()
+    ga.three()
+    ga.end()
+    spread(r.g1, r.g1, 0, 64, 0, 24, put_f32(r.wide, 64))
+    split_columns(r.wide, 3, r.w1)
+    spread(r.g1, r.g1, 0, 64, 24, 32, put_bf(r.wo1, 64))
+    r.gains[...] = r.g1[0, 64:80, :].astype(F32)[0:8]
+    gain1 = r.gains[0:1, :]
+
+    def norm(i, _):
+        x, _ = stats(r.cf[i].astype(F32).reshape(128, D))
+        r.a1[block(i), :] = (x * gain1).astype(BF)
+        return 0
+
+    four_blocks(norm)
+
+    def project(j, _):
+        r.qkv1[j] = nn(r.a1[...], r.w1[j]).astype(BF)
+        return 0
+
+    lax.fori_loop(0, 3, project, 0)
+    live = lax.broadcasted_iota(jnp.int32, (1, 512), 1) < scnt
+    backs = []
+    for k in (2, 1, 3, 0):
+        c = (s + k) % 4
+        if k:
+            attend_chunk(r.qkv1, c, live, r.o1c.at[k - 1])
+            backs.append(send(r.o1c.at[k - 1], r.o1.at[:, s], r.as2.at[k - 1], r.aq2.at[k - 1], (t, c)))
+        else:
+            attend_chunk(r.qkv1, c, live, r.o1.at[:, s])
+        if k == 2:
+            gb.one()
+        if k == 1:
+            gc.one()
+            gb.two()
+        if k == 3:
+            gc.two()
+            gb.three()
+    gb.end()
+    spread(r.g2, r.g1, 1, 64, 0, 24, put_f32(r.wide, 64))
+    split_columns(r.wide, 3, r.w2)
+    spread(r.g2, r.g1, 1, 64, 24, 32, put_bf(r.wo2, 64))
+    for copy in backs:
+        copy.wait_recv()
+    gc.three()
+    middle_forward(
+        s, r.cells, r.top, r.o1, r.wo1, r.w2, r.wo2, r.gains, scnt, fcnt, r.h1, r.h2, r.a2, r.qkv2, r.o2, r.a3, r.g
+    )
+    r.at[...] = turn(r.a3[...])
+    gc.end()
+    spread(r.g3, r.g1, 2, 128, 0, 16, put_f32(r.wide, 128))
+    split_columns(r.wide, 4, r.wup)
+
+    def put_down(i, head, last):
+        r.wdn[i // 4, pl.ds(mult((i % 4) * 128, 128), 128), :] = jnp.concatenate([head, last], 0).astype(BF)
+
+    spread(r.g3, r.g1, 2, 128, 16, 32, put_down)
+    for one in (ga, gb, gc):
+        one.drain()
+    mlp(r.a3, r.at, r.g, r.h2, r.wup, r.wdn, r.h3, r.da, r.zb, r.dub, r.u, r.dz, r.wide, r.g3)
+    edge_rows(r.g3, r.g1, 2)
+
+    def reducer(n, part, half, i):
+        bufs = [getattr(r, k) for k in reduce_names(n)]
+        return Reduce(part, *bufs, half, r.rs.at[i], r.rq.at[i], t, s)
+
+    sa, sb, sc = reducer("a", r.g1, 32, 0), reducer("b", r.g2, 32, 1), reducer("c", r.g3, 64, 2)
+    sc.core()
+    layer_output(s, r.h3, r.lout, scnt, fcnt)
+    feature_grads(
+        r.o1, r.wo1, r.w2, r.wo2, r.gains, fcnt, r.h1, r.h2, r.a2, r.qkv2, r.o2, r.g, r.da, r.b, r.do2, r.dqkv,
+        r.wide, r.g2, r.dwo1, r.do1, r.gr, r.dgain,
+    )
+    edge_rows(r.g2, r.g1, 1)
+    moves2 = [
+        send(r.do1.at[:, (s + k) % 4], r.do.at[s], r.as3.at[k - 1], r.aq3.at[k - 1], (t, (s + k) % 4))
+        for k in (1, 2, 3)
+    ]
+    r.do[s] = r.do1[:, s, :, :]
+    sb.core()
+    sc.one()
+    r.at[...] = turn(r.a1[...])
+    sb.one()
+    for copy in moves2:
+        copy.wait_recv()
+    live = lax.broadcasted_iota(jnp.int32, (512, 1), 0) < scnt
+
+    def heads(lo, hi):
+        def body(h, _):
+            backward_heads(h, r.qkv1, r.do, live, r.dqkv, r.kt, r.dkv)
+            return 0
+
+        lax.fori_loop(lo, hi, body, 0)
+
+    heads(0, 2)
+    sc.two()
+    heads(2, 3)
+    sb.two()
+    sc.three()
+    heads(3, 4)
+    sb.three()
+
+    def norm_back(i, dg):
+        rows = block(i)
+        da = nt(r.dqkv[0, rows, :], r.w1[0]) + nt(r.dqkv[1, rows, :], r.w1[1]) + nt(r.dqkv[2, rows, :], r.w1[2])
+        dh, part = norm_grad(r.cf[i].astype(F32).reshape(128, D), da, gain1)
+        r.dhs[i] = dh.astype(BF).reshape(4, 32, D)
+        return dg + part
+
+    dg = four_blocks(norm_back, jnp.zeros((1, D), F32))
+    homes = [
+        send(r.dhs.at[(s + k) % 4], r.dhr.at[:, s], r.as4.at[k - 1], r.aq4.at[k - 1], (t, (s + k) % 4))
+        for k in (1, 2, 3)
+    ]
+
+    def weights(j, _):
+        store_wide(r.wide, j, 3, nn(r.at[...], r.dqkv[j]))
+        return 0
+
+    lax.fori_loop(0, 3, weights, 0)
+
+    def narrow(i, _):
+        rows = pl.ds(mult(i * 64, 64), 64)
+        for b in range(4):
+            r.g1[i, 0:64, 128 * b : 128 * b + 128] = r.wide[b, rows, :].astype(BF)
+        return 0
+
+    lax.fori_loop(0, 24, narrow, 0)
+
+    def copy_out(i, _):
+        r.g1[24 + i, 0:64, :] = r.dwo1[pl.ds(mult(i * 64, 64), 64), :]
+        return 0
+
+    lax.fori_loop(0, 8, copy_out, 0)
+    edge_rows(r.g1, r.g1, 0)
+    edge_gains(r.g1, dg, r.dgain)
+    sa.core()
+    sa.one()
+    main3 = sc.result()
+    to_rows(main3, r.fl3)
+    main2 = sb.result()
+    to_rows(main2, r.fl2)
+    sa.two()
+    sa.three()
+    r.cgrad[:, s, :, :] = r.gr[:, s, :, :] + r.dhs[s].astype(F32)
+    for k in (1, 2, 3):
+        homes[k - 1].wait_recv()
+        f = (s + 4 - k) % 4
+        r.cgrad[:, f, :, :] = r.gr[:, f, :, :] + r.dhr[:, f, :, :].astype(F32)
+    total = sa.result()
+    to_rows(total[0:64, :], r.fl1)
+    first = total[64:72, :]
+    to_shard(first[0:1, :], r.fl1, 64, d, r.sh1)
+    to_shard(first[1:2, :], r.fl2, 64, d, r.sh2)
+    to_shard(first[2:3, :], r.fl3, 128, d, r.sh3)
+    r.sums[0] = jnp.zeros((32, 128), F32)
+    squares(r.sh1, r.m1, r.f1, r.s1, r.sums.at[0], d, 3 * D, 0)
+    squares(r.sh2, r.m2, r.f2, r.s2, r.sums.at[0], d, 3 * D, 1)
+    squares(r.sh3, r.m3, r.f3, r.s3, r.sums.at[0], d, 4 * D, 2)
+    r.total[...], adds = sum_all(r.sums, r.got, r.zs, r.ns, r.nq, t, s)
+    for one in (sa, sb, sc):
+        one.drain()
+    for copy in moves + backs + moves2 + homes + adds:
+        copy.wait_send()
+
+
+def call_m(scnt, fcnt, cells, top, params):
+    sds = jax.ShapeDtypeStruct
+    vm = pl.BlockSpec(memory_space=pltpu.VMEM)
+    sm = pl.BlockSpec(memory_space=pltpu.SMEM)
+    return pl.pallas_call(
+        kernel_m,
+        name="kernel_m",
+        out_shape=(
+            sds((4, 4, 32, D), BF), sds((4, 4, 32, D), F32), sds((264, 128), F32), sds((264, 128), F32),
+            sds((520, 128), F32), sds((32, 128), F32),
+        ),
+        in_specs=[sm, sm] + [vm] * 11,
+        out_specs=(vm,) * 6,
+        scratch_shapes=list(SCRATCH.values()),
+        compiler_params=pltpu.CompilerParams(collective_id=1, has_side_effects=True, vmem_limit_bytes=63 << 20),
+    )(scnt, fcnt, cells, top, *params)
+
+
 def local(x):
     return jnp.transpose(x.reshape(4, 32, 4, D), (0, 2, 1, 3))
 
@@ -1443,11 +1832,8 @@
 
 
 def fast_device(cells, out_grad, scnt, fcnt, b1, f1, s1, b2, f2, s2, b3, f3, s3):
-    here_cells, top = local(cells), local(out_grad)
-    o1, w1, wo1, w2, wo2, wup, wdn, gains, qkv, a1, cf = call_a(scnt, here_cells, b1, b2, b3)
-    out, gr, do1, dwo1, p2, p3, dgain = call_b(scnt, fcnt, here_cells, top, o1, wo1, w2, wo2, wup, wdn, gains)
     params = (b1, f1, s1, b2, f2, s2, b3, f3, s3)
-    cgrad, sh1, sh2, sh3, total = call_c(scnt, do1, qkv, a1, cf, w1, gains, gr, dwo1, p2, p3, dgain, params)
+    out, cgrad, sh1, sh2, sh3, total = call_m(scnt, fcnt, local(cells), local(out_grad), params)
     outs = call_e(total, (sh1, sh2, sh3), params)
     return (globe(out), globe(cgrad), *outs)
 

time: 226 us -> 198 us (0.88)
  Pallas kernels: 218 us -> 188 us
    pallas_call x3 -> x1, Pallas kernels: 212 us -> 182 us  [call_m(): pl.pallas_call(kernel_m, name='kernel_m', out_shape=(sds((4, 4, 32, D), B...]
where the time goes in v1:
time: 198 us
  Pallas kernels  188 us (95%)
  local copies, waits for them, and re-layouts  7.24 us (4%)
  between operations  2.16 us (1%)
    pallas_call x1, Pallas kernels, call_m(): pl.pallas_call(kernel_m, name='kernel_m', out_shape=(sds((4, 4, 32, D), B...  182 us
    pallas_call x1, Pallas kernels, call_e(): pl.pallas_call(kernel_e, name='kernel_e', out_shape=(*shapes, sds((9, 2),...  5.96 us

profile of v1, /device:TPU:0, one launch (start us, length us, event | category | flops | bytes accessed | tf_op | source)
XLA Modules:
  0.0 197.8 jit_solution(7853566715325708994)
XLA Ops:
  1.9 2.4 %copy_bitcast_fusion = (bf16[4,4,32,512]{3,2,1,0:T(8,128)(2,1)}, bf16[4,4,32,512]{3,2,1,0:T(8,128)(2,1)}) fusion(bf16[4,32,4,512]{3,2,1,0:T(4,128)(2,1)} %bitcast.14, bf16[4,32,4,512]{3,2,1,0:T(4,128)(2,1)} %bitcast.15), kind=kLoop, calls=%fused_computation | loop fusion | bytes 2097152 | tf_op jit(solution)/shard_map/transpose | solution.py:1827
  4.4 182.4 %kernel_m.1 = (bf16[4,4,32,512]{3,2,1,0:T(8,128)(2,1)}, f32[4,4,32,512]{3,2,1,0:T(8,128)}, f32[264,128]{1,0:T(8,128)}, f32[264,128]{1,0:T(8,128)}, f32[520,128]{1,0:T(8,128)}, /*index=5*/f32[32,128]{1,0:T(8,128)}) custom-call(s32[1]{0:T(128)S(6)} %copy.47.refs_0_, s32[1]{0:T(128)S(6)} %copy.48.refs_1_, bf16[4,4,32,512]{3,2,1,0:T(8,128)(2,1)} %get-tuple-element.99.refs_2_, ...), custom_call_target="tpu_custom_call" | custom-call | tf_op jit(solution)/shard_map/kernel_m/pallas_call | solution.py:1812
  186.8 1.2 copy.36
  188.0 1.2 copy.38
  189.2 0.0 copy-done.13
  189.2 0.1 copy.37
  189.3 0.0 copy-start
  189.3 0.0 copy-start.1
  189.3 0.0 copy-start.2
  189.3 0.0 copy-start.3
  189.3 0.0 copy-start.4
  189.3 0.0 copy-start.5
  189.3 0.0 copy-start.6
  189.3 0.0 copy-start.7
  189.4 0.0 copy-start.8
  189.4 0.0 copy-start.9
  189.4 0.0 copy-start.10
  189.4 0.0 copy-start.12
  189.4 1.6 copy.39
  191.0 0.0 copy-done.11
  191.1 0.0 copy-done.3
  191.1 0.0 copy-done.4
  191.1 6.0 %kernel_e.1 = (f32[32784]{0:T(1024)}, f32[32784]{0:T(1024)}, f32[32784]{0:T(1024)}, f32[32784]{0:T(1024)}, bf16[32784]{0:T(1024)(128)(2,1)}, /*index=5*/f32[3278...) custom-call(f32[32,128]{1,0:T(8,128)S(1)} %copy-done.12, ...), custom_call_target="tpu_custom_call" | custom-call | tf_op jit(solution)/shard_map/kernel_e/pallas_call | solution.py:827
  197.1 0.6 copy.40
  (12 shorter events, 0.0 us)
Async XLA Ops:
  186.8 2.4 %copy-start.13 = (f32[4,4,32,512]{3,2,1,0:T(8,128)S(1)}, f32[4,4,32,512]{3,2,1,0:T(8,128)}, u32[]{:S(2)}) copy-start(f32[4,4,32,512]{3,2,1,0:T(8,128)} %get-tuple-element.41) | copy-start | bytes 3145732
  189.2 1.9 copy-start.11
  189.3 1.8 copy-start
  189.3 1.8 copy-start.1
  189.3 1.8 copy-start.2
  189.3 1.8 copy-start.3
  189.3 1.8 copy-start.4
  189.3 1.8 copy-start.5
  189.3 1.8 copy-start.6
  189.3 1.8 copy-start.7
  189.4 1.8 copy-start.8
  189.4 1.8 copy-start.9
  189.4 1.8 copy-start.10
  189.4 1.8 copy-start.12
